TPU v7x, 32 devices: a whole 2x2x4 slice. The times are simulated.
32 devices in a mesh: seq: 4 (over z), exp: 8 (over y, x, core).
Axes of the slice: x: 2, y: 2, z: 4, core: 2. Of those that a mesh axis runs over, the one named last changes fastest.
Arguments:
- queries: bfloat16 [8, 16, 8192], P('exp', 'seq'), may hold values from -8 to 8
- key_rows: bfloat16 [8, 16, 512], P('exp', 'seq'), may hold values from -8 to 8
- values: bfloat16 [8, 16, 512], P('exp', 'seq'), may hold values from -6 to 6
- residual: bfloat16 [8, 16, 4096], P('exp'), may hold values from -4 to 4
- out_proj: bfloat16 [8192, 4096], P('seq'), may hold values from -0.25 to 0.25
- norm_gain: bfloat16 [4096], replicated, may hold values from 0.5 to 1.5
- expert_ids: int32 [8, 16, 8], P('exp'), may hold values from 0 to 15, all different within a row; in each aligned block of 16 rows (0 to 15, 16 to 31, ..., all dimensions but the last counted through in order) at most 10 rows name the same one
- route_weights: float32 [8, 16, 8], P('exp'), may hold values from 0.05 to 0.35
- gate_weight: bfloat16 [4, 8, 4096, 512], P('seq', 'exp'), may hold values from -0.09375 to 0.09375
- up_weight: bfloat16 [4, 8, 4096, 512], P('seq', 'exp'), may hold values from -0.09375 to 0.09375
- down_weight: bfloat16 [16, 1024, 4096], P('exp', None, 'seq'), may hold values from -0.1875 to 0.1875
Outputs:
- layer_out: bfloat16 [8, 16, 4096], P('exp', None, 'seq')
Inputs may be any that keep to these rules, and one draw needn't show every extreme that they name: `expert_ids`: each token names 8 different experts. In each query block no expert is named by more than 10 of its tokens, and in some block an expert is named by exactly 10.
All inputs are finite; a program needn't handle non-finite values.
Results may differ from a plain program's by a relative error of at most 0.018.
Values may be sent and summed in bfloat16 or wider, within the bound.
No kernel may reach another device: no remote copies, remote signals or barrier semaphores. Data moves between devices by JAX's collectives and lax.ppermute only.
A program may use at most 64 MiB of HBM per device.

v0:
```python
import jax
import jax.numpy as jnp
from jax import lax
from jax.sharding import PartitionSpec as P

D = 4096
HEADS = 64
KV_HEADS = 4
HEAD_DIM = 128
FF = 1024
TOPK = 8
EXP_DEV = 2


norm_eps = 1e-06
masked_score = -1e30


def shards(
    queries,
    key_rows,
    values,
    residual,
    out_proj,
    norm_gain,
    expert_ids,
    route_weights,
    gate_weight,
    up_weight,
    down_weight,
):
    seq_count = lax.axis_size("seq")
    exp_count = lax.axis_size("exp")
    seq_index = lax.axis_index("seq")
    exp_index = lax.axis_index("exp")
    tok_dev = queries.shape[1]
    column = tok_dev * seq_count
    head_dev = HEADS // seq_count
    score_scale = HEAD_DIM ** (-0.5)
    q_local = queries.reshape(tok_dev, seq_count, head_dev * HEAD_DIM)
    k_local = key_rows.reshape(tok_dev, KV_HEADS, HEAD_DIM)
    v_local = values.reshape(tok_dev, KV_HEADS, HEAD_DIM)
    pair_local = jnp.repeat(
        jnp.concatenate([k_local, v_local], axis=2), seq_count // KV_HEADS, axis=1
    )
    q_column, pair_column = (
        lax.all_to_all(q_local, "seq", split_axis=1, concat_axis=0, tiled=True),
        lax.all_to_all(pair_local, "seq", split_axis=1, concat_axis=0, tiled=True),
    )
    q_heads = q_column.reshape(column, head_dev, HEAD_DIM)
    pair_column = pair_column.reshape(column, 2 * HEAD_DIM)
    query_pos = exp_index * column + lax.iota(jnp.int32, column)
    last_query = exp_index * column + (column - 1)
    starting = (
        jnp.full((head_dev, column), masked_score, jnp.float32),
        jnp.zeros((head_dev, column), jnp.float32),
        jnp.zeros((head_dev, column, HEAD_DIM), jnp.float32),
    )
    shard_pair = lax.all_gather(pair_column, "exp", axis=0, tiled=True)

    def update(current):
        top_score, weight_sum, accumulated = current
        key_part = shard_pair[:, :HEAD_DIM]
        value_part = shard_pair[:, HEAD_DIM:]
        scores = (
            jnp.einsum("qhd,kd->hqk", q_heads, key_part, preferred_element_type=jnp.float32)
            * score_scale
        )
        key_pos = lax.iota(jnp.int32, shard_pair.shape[0])
        allowed = key_pos[None, :] <= query_pos[:, None]
        scores = jnp.where(allowed[None], scores, masked_score)
        new_top = jnp.maximum(top_score, jnp.max(scores, axis=2))
        weights = jnp.where(allowed[None], jnp.exp(scores - new_top[:, :, None]), 0.0)
        weight_sum = jnp.sum(weights, axis=2)
        accumulated = jnp.einsum(
            "hqk,kd->hqd",
            weights.astype(jnp.bfloat16),
            value_part,
            preferred_element_type=jnp.float32,
        )
        return (new_top, weight_sum, accumulated)

    def unchanged(current):
        return current

    top_score, weight_sum, accumulated = lax.cond(
        jnp.int32(0) <= last_query, update, unchanged, starting
    )
    attended = (accumulated / weight_sum[:, :, None]).astype(jnp.bfloat16)
    projected = jnp.einsum(
        "hqd,hde->qe",
        attended,
        out_proj.reshape(head_dev, HEAD_DIM, D),
        preferred_element_type=jnp.float32,
    )
    col_width = down_weight.shape[2]
    summed = lax.psum(projected.astype(jnp.bfloat16), "seq").astype(jnp.float32)
    hidden_one = residual[0].astype(jnp.float32) + summed
    mean_square = jnp.mean(hidden_one * hidden_one, axis=1, keepdims=True)
    normed = (
        hidden_one * lax.rsqrt(mean_square + norm_eps) * norm_gain.astype(jnp.float32)
    ).astype(jnp.bfloat16)
    kept = lax.dynamic_slice_in_dim(hidden_one, seq_index * col_width, col_width, 1)
    experts = EXP_DEV * exp_count
    capacity = min(column, column * TOPK // experts + 2)
    route_ids = expert_ids[0]
    flat_ids = route_ids.reshape(-1)
    onehot = (flat_ids[:, None] == lax.iota(jnp.int32, experts)[None, :]).astype(jnp.int32)
    slot_of = (jnp.sum(jnp.cumsum(onehot, axis=0) * onehot, axis=1) - 1).reshape(column, TOPK)
    slices = seq_count // 2
    parity = seq_index // slices
    target = route_ids // 2 * capacity + slot_of
    chosen = route_ids % 2 == parity
    places = lax.iota(jnp.int32, exp_count * capacity)
    dispatch_map = jnp.any(
        (target[:, :, None] == places[None, None, :]) & chosen[:, :, None], axis=1
    ).astype(jnp.bfloat16)
    gate_local = gate_weight[0, 0]
    up_local = up_weight[0, 0]
    rows_full = jnp.einsum("tp,td->pd", dispatch_map, normed, preferred_element_type=jnp.float32)
    rows_full = rows_full.astype(jnp.bfloat16).reshape(exp_count, capacity, D)
    rows_in = lax.all_to_all(rows_full, "exp", split_axis=0, concat_axis=0, tiled=True)
    gate_vals = jnp.einsum("ecd,df->ecf", rows_in, gate_local, preferred_element_type=jnp.float32)
    up_vals = jnp.einsum("ecd,df->ecf", rows_in, up_local, preferred_element_type=jnp.float32)
    activated = (jax.nn.silu(gate_vals) * up_vals).astype(jnp.bfloat16)
    whole = lax.all_gather(activated, "seq", axis=2, tiled=True)
    first = jnp.einsum(
        "ecf,fo->eco", whole[:, :, :FF], down_weight[0], preferred_element_type=jnp.float32
    )
    second = jnp.einsum(
        "ecf,fo->eco", whole[:, :, FF:], down_weight[1], preferred_element_type=jnp.float32
    )
    outputs = jnp.stack([first, second], axis=2).astype(jnp.bfloat16)
    returned = lax.all_to_all(outputs, "exp", split_axis=0, concat_axis=0, tiled=True)
    index_map = route_ids // 2 * (capacity * 2) + slot_of * 2 + route_ids % 2
    positions = lax.iota(jnp.int32, exp_count * capacity * 2)
    combine_table = jnp.sum(
        jnp.where(
            index_map[:, :, None] == positions[None, None, :], route_weights[0][:, :, None], 0.0
        ),
        axis=1,
    )
    routed = jnp.dot(
        combine_table,
        returned.astype(jnp.float32).reshape(exp_count * capacity * 2, col_width),
        precision=lax.Precision.HIGHEST,
        preferred_element_type=jnp.float32,
    )
    return (kept + routed).astype(jnp.bfloat16)[None]


def solution(mesh):
    in_specs = (
        P("exp", "seq", None),
        P("exp", "seq", None),
        P("exp", "seq", None),
        P("exp", None, None),
        P("seq", None),
        P(),
        P("exp", None, None),
        P("exp", None, None),
        P("seq", "exp", None, None),
        P("seq", "exp", None, None),
        P("exp", None, "seq"),
    )
    out_specs = P("exp", None, "seq")
    return jax.shard_map(shards, mesh=mesh, in_specs=in_specs, out_specs=out_specs, check_vma=False)
```

profile of v0, /device:TPU:0, one launch (start us, length us, event | category | flops | bytes accessed | tf_op | source)
XLA Modules:
  0.0 138.9 jit_solution(839728186197407362)
XLA Ops:
  6.5 1.3 pad_maximum_fusion.1
  7.8 6.3 %all-to-all-start = ((bf16[4,4,256]{2,0,1:T(4,128)(2,1)}), bf16[4,4,256]{2,0,1:T(4,128)(2,1)S(1)}, u32[]{:S(2)}, u32[]{:S(2)}) async-start(bf16[4,4,256]{2,0,1:T(4,128)(2,1)} %pad_maximum_fusion.1), calls=%async_computation | async-start | bytes 16384 | tf_op jit(solution)/shard_map/all_to_all | solution.py:48
  14.2 0.8 copy.49
  15.0 0.1 fusion.45
  15.1 0.2 reduce_window_sum.11
  15.3 0.2 select_reduce_fusion.1
  15.6 4.1 %all-to-all-done = bf16[4,4,256]{2,0,1:T(4,128)(2,1)S(1)} async-done(((bf16[4,4,256]{2,0,1:T(4,128)(2,1)}), bf16[4,4,256]{2,0,1:T(4,128)(2,1)S(1)}, u32[]{:S(2)}, u32[]{:S(2)}) %all-to-all-start) | async-done | bytes 8224 | tf_op jit(solution)/shard_map/all_to_all | solution.py:48
  19.8 3.3 %all-to-all-start.1 = ((bf16[4,4,2048]{2,0,1:T(4,128)(2,1)}), bf16[4,4,2048]{2,0,1:T(4,128)(2,1)S(1)}, u32[]{:S(2)}, u32[]{:S(2)}) async-start(bf16[4,4,2048]{2,0,1:T(4,128)(2,1)} %bitcast.118), calls=%async_computation.1 | async-start | bytes 131072 | tf_op jit(solution)/shard_map/all_to_all | solution.py:47
  23.1 0.7 multiply_add_fusion
  23.9 9.3 %all_gather.6 = bf16[128,256]{1,0:T(8,128)(2,1)S(1)} all-gather(bf16[16,256]{1,0:T(8,128)(2,1)S(1)} %reshape.147), channel_id=1, replica_groups=mesh['seq'=4,'exp'=8] {'exp'}, dimensions={0}, use_global_device_ids=true | all-gather | bytes 73728 | tf_op jit(solution)/shard_map/all_gather | solution.py:59
  33.1 0.8 conditional.1
  33.3 0.3 fusion.52
  33.5 0.2 fusion.2
  33.7 0.1 fusion.4
  34.0 7.7 %fusion.10 = bf16[16,4096]{1,0:T(8,128)(2,1)} fusion(bf16[16,128,4096]{2,1,0:T(8,128)(2,1)} %bitcast.116, f32[16,16,128]{2,1,0:T(8,128)S(1)} %get-tuple-element.22, f32[16,16]{1,0:T(8,128)S(1)} %copy.48), kind=kOutput, calls=%fused_computation.17 | convolution fusion | flops 268566528 | bytes 17040384 | tf_op jit(solution)/shard_map/hqd,hde->qe/dot_general | solution.py:90
  41.9 0.1 fusion.48
  42.0 34.9 %all-reduce.2.cloned.1.call-done = bf16[16,4096]{1,0:T(8,128)(2,1)} async-done(((bf16[16,4096]{1,0:T(8,128)(2,1)}), bf16[16,4096]{1,0:T(8,128)(2,1)}) %all-reduce.2.cloned.1.call-update) | async-done | bytes 131088 | tf_op jit(solution)/shard_map/psum | solution.py:97
  76.9 1.1 convert_add_fusion
  78.0 1.3 convolution_convert_fusion
  79.3 0.2 reshape.150
  79.5 19.0 %all_to_all.40 = bf16[8,10,4096]{2,1,0:T(8,128)(2,1)S(1)} all-to-all(bf16[8,10,4096]{2,1,0:T(8,128)(2,1)S(1)} %reshape.150), channel_id=1, replica_groups=mesh['seq'=4,'exp'=8] {'exp'}, dimensions={0} | all-to-all | bytes 1310720 | tf_op jit(solution)/shard_map/all_to_all | solution.py:122
  98.6 3.0 %fusion.13 = f32[8,10,512]{2,1,0:T(8,128)S(1)} fusion(bf16[8,10,4096]{2,1,0:T(8,128)(2,1)S(1)} %all_to_all.40, bf16[1,1,4096,512]{3,2,1,0:T(8,128)(2,1)} %param.21), kind=kOutput, calls=%fused_computation.20 | convolution fusion | flops 335544320 | bytes 5013504 | tf_op jit(solution)/shard_map/ecd,df->ecf/dot_general | solution.py:123
  101.6 0.7 fusion.36
  102.3 15.7 %all_gather.7 = bf16[8,10,2048]{2,1,0:T(8,128)(2,1)S(1)} all-gather(bf16[8,10,512]{2,1,0:T(8,128)(2,1)S(1)} %fusion.36), channel_id=1, replica_groups=mesh['seq'=4,'exp'=8] {'seq'}, dimensions={2}, use_global_device_ids=true | all-gather | bytes 409600 | tf_op jit(solution)/shard_map/all_gather | solution.py:126
  118.0 0.5 fusion.27
  118.5 0.5 fusion.30
  119.0 1.0 copy.56
  120.1 3.4 %all-to-all-start.3 = ((bf16[8,10,2,1024]{3,2,1,0:T(2,128)(2,1)}), bf16[8,10,2,1024]{3,2,1,0:T(2,128)(2,1)S(1)}, u32[]{:S(2)}, u32[]{:S(2)}) async-start(bf16[8,10,2,1024]{3,2,1,0:T(2,128)(2,1)} %copy.56), calls=%async_computation.3 | async-start | bytes 655360 | tf_op jit(solution)/shard_map/all_to_all | solution.py:134
  123.6 0.1 select_reduce_fusion
  123.8 7.3 %all-to-all-done.3 = bf16[8,10,2,1024]{3,2,1,0:T(2,128)(2,1)S(1)} async-done(((bf16[8,10,2,1024]{3,2,1,0:T(2,128)(2,1)}), bf16[8,10,2,1024]{3,2,1,0:T(2,128)(2,1)S(1)}, u32[]{:S(2)}, u32[]{:S(2)}) %all-to-all-start.3) | async-done | bytes 327712 | tf_op jit(solution)/shard_map/all_to_all | solution.py:134
  131.0 0.1 reshape.151
  131.2 0.9 fusion.40
  (34 shorter events, 0.9 us)
Async XLA Ops:
  7.8 11.9 %all-to-all-start = ((bf16[4,4,256]{2,0,1:T(4,128)(2,1)}), bf16[4,4,256]{2,0,1:T(4,128)(2,1)S(1)}, u32[]{:S(2)}, u32[]{:S(2)}) async-start(bf16[4,4,256]{2,0,1:T(4,128)(2,1)} %pad_maximum_fusion.1), calls=%async_computation | async-start | bytes 16384 | tf_op jit(solution)/shard_map/all_to_all | solution.py:48
  19.8 13.3 %all-to-all-start.1 = ((bf16[4,4,2048]{2,0,1:T(4,128)(2,1)}), bf16[4,4,2048]{2,0,1:T(4,128)(2,1)S(1)}, u32[]{:S(2)}, u32[]{:S(2)}) async-start(bf16[4,4,2048]{2,0,1:T(4,128)(2,1)} %bitcast.118), calls=%async_computation.1 | async-start | bytes 131072 | tf_op jit(solution)/shard_map/all_to_all | solution.py:47
  23.1 53.9 %all-reduce.2.cloned.1.call-start = ((), (), s32[]{:S(2)}) async-start(), calls=%async_computation.4 | async-start | bytes 262144 | tf_op jit(solution)/shard_map/psum | solution.py:97
  34.0 7.8 %copy-start.1 = (s32[1,16,8]{1,2,0:T(8,128)S(1)}, s32[1,16,8]{1,2,0:T(8,128)}, u32[]{:S(2)}) copy-start(s32[1,16,8]{1,2,0:T(8,128)} %param.19) | copy-start | bytes 1540
  34.0 7.9 %copy-start.2 = (bf16[4096]{0:T(1024)(128)(2,1)S(1)}, bf16[4096]{0:T(1024)(128)(2,1)}, u32[]{:S(2)}) copy-start(bf16[4096]{0:T(1024)(128)(2,1)} %param.18) | copy-start | bytes 24580
  34.0 43.0 %copy-start = (bf16[1,16,4096]{2,1,0:T(8,128)(2,1)S(1)}, bf16[1,16,4096]{2,1,0:T(8,128)(2,1)}, u32[]{:S(2)}) copy-start(bf16[1,16,4096]{2,1,0:T(8,128)(2,1)} %param.16) | copy-start | bytes 393220
  79.5 22.0 %copy-start.4 = (bf16[1,1,4096,512]{3,2,1,0:T(8,128)(2,1)S(1)}, bf16[1,1,4096,512]{3,2,1,0:T(8,128)(2,1)}, u32[]{:S(2)}) copy-start(bf16[1,1,4096,512]{3,2,1,0:T(8,128)(2,1)} %param.22) | copy-start | bytes 12582916
  101.5 16.5 %copy-start.5 = (bf16[2,1024,1024]{2,1,0:T(8,128)(2,1)S(1)}, bf16[2,1024,1024]{2,1,0:T(8,128)(2,1)}, u32[]{:S(2)}) copy-start(bf16[2,1024,1024]{2,1,0:T(8,128)(2,1)} %param.23) | copy-start | bytes 12582916
  118.0 5.6 %copy-start.3 = (f32[1,16,8]{1,2,0:T(8,128)S(1)}, f32[1,16,8]{1,2,0:T(8,128)}, u32[]{:S(2)}) copy-start(f32[1,16,8]{1,2,0:T(8,128)} %param.20) | copy-start | bytes 1540
  120.1 11.0 %all-to-all-start.3 = ((bf16[8,10,2,1024]{3,2,1,0:T(2,128)(2,1)}), bf16[8,10,2,1024]{3,2,1,0:T(2,128)(2,1)S(1)}, u32[]{:S(2)}, u32[]{:S(2)}) async-start(bf16[8,10,2,1024]{3,2,1,0:T(2,128)(2,1)} %copy.56), calls=%async_computation.3 | async-start | bytes 655360 | tf_op jit(solution)/shard_map/all_to_all | solution.py:134
Sparse Core Ops, SparseCore 0:
  41.8 35.0 all-reduce.1
where the time goes:
time: 139 us
  waiting for transfers between devices  46.3 us (33%)
  blocking collectives  44 us (32%)
  matrix products  14.9 us (11%)
  between operations  13.6 us (10%)
  starting transfers between devices  13.1 us (9%)
  other arithmetic  4.12 us (3%)
  local copies, waits for them, and re-layouts  2.85 us (2%)
    psum x1, waiting for transfers between devices, shards(): summed = lax.psum(projected.astype(jnp.bfloat16), 'seq').astype(jnp.float32)  34.9 us
    all_to_all x1, blocking collectives, shards(): lax.all_to_all(rows_full, 'exp', split_axis=0, concat_axis=0, tiled=True)  19 us
    all_gather x1, blocking collectives, shards(): whole = lax.all_gather(activated, 'seq', axis=2, tiled=True)  15.7 us
    all_gather x1, blocking collectives, shards(): shard_pair = lax.all_gather(pair_column, 'exp', axis=0, tiled=True)  9.26 us
    dot_general x1, matrix products, shards(): jnp.einsum('hqd,hde->qe', attended, out_proj.reshape(head_dev, HEAD_DIM,...  7.72 us
    all_to_all x1, waiting for transfers between devices, shards(): lax.all_to_all(outputs, 'exp', split_axis=0, concat_axis=0, tiled=True)  7.26 us
    all_to_all x1, starting transfers between devices, shards(): lax.all_to_all(pair_local, 'seq', split_axis=1, concat_axis=0, tiled=True)  6.35 us
    all_to_all x1, waiting for transfers between devices, shards(): lax.all_to_all(pair_local, 'seq', split_axis=1, concat_axis=0, tiled=True)  4.13 us
  transfers between devices with their start and end apart: 4, of which 3 were waited for; matrix products, arithmetic and copies ran while one was open for 2% of the time, Pallas kernels for 0%

commit v1 on v0

--- a/solution.py
+++ b/solution.py
@@ -14,6 +14,169 @@
 
 norm_eps = 1e-06
 masked_score = -1e30
+
+def exchange(value, axis, step):
+    count = lax.axis_size(axis)
+    return lax.ppermute(value, axis, [(i, i ^ step) for i in range(count)])
+
+
+def in_order(pieces, index):
+    bit = 1
+    while bit < len(pieces):
+        swap = (index & bit) != 0
+        pieces = [jnp.where(swap, pieces[i ^ bit], pieces[i]) for i in range(len(pieces))]
+        bit *= 2
+    return pieces
+
+
+def compact(
+    queries,
+    key_rows,
+    values,
+    residual,
+    out_proj,
+    norm_gain,
+    expert_ids,
+    route_weights,
+    gate_weight,
+    up_weight,
+    down_weight,
+):
+    seq_count = lax.axis_size("seq")
+    exp_count = lax.axis_size("exp")
+    s = lax.axis_index("seq")
+    e = lax.axis_index("exp")
+    bf16, f32 = jnp.bfloat16, jnp.float32
+    tok_dev = queries.shape[1]
+    column = tok_dev * seq_count
+    head_dev = HEADS // seq_count
+    exp_dev = down_weight.shape[0]
+    experts = exp_dev * exp_count
+    steps = list(range(0, exp_count, 2)) + list(range(1, exp_count, 2))
+    half = exp_count // 2
+    tokens = exp_count * column
+
+    q_local = queries.reshape(tok_dev, seq_count, head_dev * HEAD_DIM)
+    k_local = key_rows.reshape(tok_dev, KV_HEADS, HEAD_DIM)
+    v_local = values.reshape(tok_dev, KV_HEADS, HEAD_DIM)
+    reps = seq_count // KV_HEADS
+    wide = jnp.concatenate(
+        [q_local, jnp.repeat(k_local, reps, axis=1), jnp.repeat(v_local, reps, axis=1)], axis=2
+    )
+    pieces = []
+    for k in range(seq_count):
+        piece = lax.dynamic_index_in_dim(wide, s ^ k, 1, keepdims=False)
+        pieces.append(piece if k == 0 else exchange(piece, "seq", k))
+    rows = jnp.concatenate(in_order(pieces, s), axis=0)
+    q_heads = rows[:, : head_dev * HEAD_DIM].reshape(column * head_dev, HEAD_DIM)
+
+    expert_of = lax.iota(jnp.int32, experts)
+    table = jnp.sum(
+        jnp.where(
+            expert_ids[0][:, :, None] == expert_of[None, None, :], route_weights[0][:, :, None], 0.0
+        ),
+        axis=1,
+    )
+    high = lax.reduce_precision(table, 8, 7)
+    middle = lax.reduce_precision(table - high, 8, 7)
+    low = table - high - middle
+    lanes = 128
+    packed = jnp.concatenate([high, middle, low], axis=1).astype(bf16)
+    packed = jnp.pad(packed, ((0, 0), (0, -packed.shape[1] % lanes)))
+    block = jnp.concatenate([rows[:, head_dev * HEAD_DIM :], packed], axis=1)
+    near = jnp.concatenate(
+        [block] + [exchange(block, "exp", k) for k in range(2, exp_count, 2)], axis=0
+    )
+    gathered = jnp.concatenate([near, exchange(near, "exp", 1)], axis=0)
+    keys = gathered[:, :HEAD_DIM]
+    vals = gathered[:, HEAD_DIM : 2 * HEAD_DIM]
+    terms = gathered[:, 2 * HEAD_DIM : 2 * HEAD_DIM + 3 * experts].astype(f32)
+    weight_of = terms[:, :experts] + terms[:, experts : 2 * experts] + terms[:, 2 * experts :]
+
+    position = lax.iota(jnp.int32, tokens)
+    step_of = position // column
+    step_of = jnp.where(step_of < half, 2 * step_of, 2 * (step_of - half) + 1)
+    key_pos = (e ^ step_of) * column + position % column
+    query_pos = e * column + lax.iota(jnp.int32, column * head_dev) // head_dev
+    scores = jnp.dot(q_heads, keys.T, preferred_element_type=f32) * (HEAD_DIM ** (-0.5))
+    allowed = key_pos[None, :] <= query_pos[:, None]
+    scores = jnp.where(allowed, scores, masked_score)
+    top = jnp.max(scores, axis=1, keepdims=True)
+    weights = jnp.where(allowed, jnp.exp(scores - top), 0.0)
+    total = jnp.sum(weights, axis=1, keepdims=True)
+    attended = jnp.dot(weights.astype(bf16), vals, preferred_element_type=f32) / total
+    attended = attended.astype(bf16).reshape(column, head_dev * HEAD_DIM)
+    projected = jnp.dot(attended, out_proj, preferred_element_type=f32)
+    step = 1
+    while step < seq_count:
+        projected = projected + exchange(projected.astype(bf16), "seq", step).astype(f32)
+        step *= 2
+    hidden_one = residual[0].astype(f32) + projected
+    mean_square = jnp.mean(hidden_one * hidden_one, axis=1, keepdims=True)
+    normed = (hidden_one * lax.rsqrt(mean_square + norm_eps) * norm_gain.astype(f32)).astype(bf16)
+    col_width = down_weight.shape[2]
+    kept = lax.dynamic_slice_in_dim(hidden_one, s * col_width, col_width, 1)
+
+    capacity = min(column, column * TOPK // experts + 2)
+    slots = exp_count * capacity
+    mine = lax.dynamic_slice_in_dim(weight_of, e * exp_dev, exp_dev, 1)
+    named = (mine != 0.0).astype(bf16)
+    before = (
+        (position[None, :] < position[:, None])
+        & (position[None, :] // column == position[:, None] // column)
+    ).astype(bf16)
+    rank = jnp.dot(before, named, preferred_element_type=f32).astype(jnp.int32)
+    slot = jnp.where(mine != 0.0, (position // column * capacity)[:, None] + rank, -1)
+    slot_of = lax.iota(jnp.int32, slots)
+    parity = s // (seq_count // exp_dev)
+    own_slot = jnp.sum(jnp.where(lax.iota(jnp.int32, exp_dev)[None, :] == parity, slot, 0), axis=1)
+    pick = (slot_of[:, None] == own_slot[None, :]).astype(bf16)
+    combine = jnp.concatenate(
+        [
+            jnp.where(slot_of[None, :] == slot[:, p : p + 1], mine[:, p : p + 1], 0.0)
+            for p in range(exp_dev)
+        ],
+        axis=1,
+    )
+
+    near = jnp.concatenate(
+        [normed] + [exchange(normed, "exp", k) for k in range(2, exp_count, 2)], axis=0
+    )
+    far = exchange(near, "exp", 1)
+    gate_local = gate_weight[0, 0]
+    up_local = up_weight[0, 0]
+
+    def units(part):
+        gate_vals = jnp.dot(part, gate_local, preferred_element_type=f32)
+        up_vals = jnp.dot(part, up_local, preferred_element_type=f32)
+        return (jax.nn.silu(gate_vals) * up_vals).astype(bf16)
+
+    activated = units(jnp.concatenate([near, far], axis=0))
+    activated = jnp.dot(pick, activated, preferred_element_type=f32).astype(bf16)
+    pieces = [activated] + [exchange(activated, "seq", k) for k in range(1, seq_count)]
+    pieces = in_order(pieces, s)
+    group = seq_count // exp_dev
+    outputs = jnp.concatenate(
+        [
+            jnp.dot(
+                jnp.concatenate(pieces[p * group : (p + 1) * group], axis=1),
+                down_weight[p],
+                preferred_element_type=f32,
+            )
+            for p in range(exp_dev)
+        ],
+        axis=0,
+    ).astype(bf16)
+    routed = jnp.dot(
+        combine, outputs.astype(f32), precision=lax.Precision.HIGHEST, preferred_element_type=f32
+    )
+    mid = half * column
+    routed = routed[:mid] + exchange(routed[mid:].astype(bf16), "exp", 1).astype(f32)
+    result = kept + routed[:column]
+    for i in range(1, half):
+        part = routed[i * column : (i + 1) * column].astype(bf16)
+        result = result + exchange(part, "exp", 2 * i).astype(f32)
+    return result.astype(bf16)[None]
 
 
 def shards(
@@ -31,6 +194,20 @@
 ):
     seq_count = lax.axis_size("seq")
     exp_count = lax.axis_size("exp")
+    if down_weight.shape[0] * exp_count <= 2 * TOPK:
+        return compact(
+            queries,
+            key_rows,
+            values,
+            residual,
+            out_proj,
+            norm_gain,
+            expert_ids,
+            route_weights,
+            gate_weight,
+            up_weight,
+            down_weight,
+        )
     seq_index = lax.axis_index("seq")
     exp_index = lax.axis_index("exp")
     tok_dev = queries.shape[1]

time: 139 us -> 84.6 us (0.61)
  blocking collectives: 44 us -> 0 us
  between operations: 13.6 us -> 0.38 us
  waiting for transfers between devices: 46.3 us -> 36 us
  starting transfers between devices: 13.1 us -> 23.3 us
  matrix products: 14.9 us -> 17.3 us
  local copies, waits for them, and re-layouts: 2.85 us -> 4.59 us
  other arithmetic: 4.12 us -> 2.58 us
    ppermute x0 -> x20, waiting for transfers between devices: none -> 36 us  [exchange(): return lax.ppermute(value, axis, [(i, i ^ step) for i in range(count)])]
    psum x1 -> x0, waiting for transfers between devices: 34.9 us -> none  [shards(): summed = lax.psum(projected.astype(jnp.bfloat16), 'seq').astype(jnp.float32)]
    all_gather x2 -> x0, blocking collectives: 25 us -> none  [the longest x1 15.7 us: shards(): whole = lax.all_gather(activated, 'seq', axis=2, tiled=True)]
    ppermute x0 -> x20, starting transfers between devices: none -> 23.3 us  [exchange(): return lax.ppermute(value, axis, [(i, i ^ step) for i in range(count)])]
    all_to_all x1 -> x0, blocking collectives: 19 us -> none  [shards(): lax.all_to_all(rows_full, 'exp', split_axis=0, concat_axis=0, tiled=True)]
    all_to_all x3 -> x0, starting transfers between devices: 13.1 us -> none  [the longest x1 6.35 us: shards(): lax.all_to_all(pair_local, 'seq', split_axis=1, concat_axis=0, tiled=True)]
    all_to_all x3 -> x0, waiting for transfers between devices: 11.4 us -> none  [the longest x1 7.26 us: shards(): lax.all_to_all(outputs, 'exp', split_axis=0, concat_axis=0, tiled=True)]
    dot_general x9, matrix products: 14.9 us -> 17.3 us  [the longest x1 8.09 us: compact(): projected = jnp.dot(attended, out_proj, preferred_element_type=f32)]
  transfers between devices with their start and end apart: 4 -> 20, of which waited for: 3 -> 16; matrix products, arithmetic and copies ran while one was open for 2% -> 4% of each run, Pallas kernels for 0% -> 0%
where the time goes in v1:
time: 84.6 us; the launch traced here: 84.2 us
  waiting for transfers between devices  36 us (43%)
  starting transfers between devices  23.3 us (28%)
  matrix products  17.3 us (20%)
  local copies, waits for them, and re-layouts  4.59 us (5%)
  other arithmetic  2.58 us (3%)
    ppermute x20, waiting for transfers between devices, exchange(): return lax.ppermute(value, axis, [(i, i ^ step) for i in range(count)])  36 us
    ppermute x20, starting transfers between devices, exchange(): return lax.ppermute(value, axis, [(i, i ^ step) for i in range(count)])  23.3 us
    dot_general x1, matrix products, compact(): projected = jnp.dot(attended, out_proj, preferred_element_type=f32)  8.09 us
    dot_general x2, matrix products, compact(): jnp.dot(jnp.concatenate(pieces[p * group:(p + 1) * group], axis=1), down_...  4.16 us
    dot_general x1, matrix products, compact(): jnp.dot(pick, activated, preferred_element_type=f32).astype(bf16)  3.1 us
  transfers between devices with their start and end apart: 20, of which 16 were waited for; matrix products, arithmetic and copies ran while one was open for 4% of the time, Pallas kernels for 0%

profile of v1, /device:TPU:0, one launch (start us, length us, event | category | flops | bytes accessed | tf_op | source)
XLA Modules:
  0.0 84.2 jit_solution(3526082246969393240)
XLA Ops:
  0.0 0.9 %reshape.139 = bf16[4,4,2048]{2,1,0:T(4,128)(2,1)S(1)} reshape(bf16[1,4,8192]{2,1,0:T(4,128)(2,1)} %param.11) | data formatting | bytes 131072 | tf_op jit(solution)/shard_map/reshape | solution.py:59
  2.6 5.1 %collective-permute-start = (bf16[4,2304]{1,0:T(4,128)(2,1)S(1)}, bf16[4,2304]{1,0:T(4,128)(2,1)S(1)}, u32[]{:S(2)}, u32[]{:S(2)}) collective-permute-start(bf16[4,2304]{1,0:T(4,128)(2,1)S(1)} %bitcast.55), channel_id=1, source_target_pairs={{0,24},{8,16},{16,8},{24,0},{1,25},{9,17},{17,9},{25,1},{2,26},{10... | collective-permute-start | bytes 55304 | tf_op jit(solution)/shard_map/ppermute | solution.py:20
  8.4 0.8 copy.38
  9.2 0.8 copy.37
  10.2 2.2 %collective-permute-done.1 = bf16[4,2304]{1,0:T(4,128)(2,1)S(1)} collective-permute-done((bf16[4,2304]{1,0:T(4,128)(2,1)S(1)}, bf16[4,2304]{1,0:T(4,128)(2,1)S(1)}, u32[]{:S(2)}, u32[]{:S(2)}) %collective-permute-start.1) | collective-permute-done | bytes 18464 | tf_op jit(solution)/shard_map/ppermute | solution.py:20
  12.7 1.6 %collective-permute-start.3 = (bf16[16,384]{0,1:T(8,128)(2,1)S(1)}, bf16[16,384]{0,1:T(8,128)(2,1)S(1)}, u32[]{:S(2)}, u32[]{:S(2)}) collective-permute-start(bf16[16,384]{0,1:T(8,128)(2,1)S(1)} %copy.43), channel_id=1, source_target_pairs={{0,2},{1,3},{2,0},{3,1},{4,6},{5,7},{6,4},{7,5},{8,10},{9,11},{10,... | collective-permute-start | bytes 36872 | tf_op jit(solution)/shard_map/ppermute | solution.py:20
  14.2 1.5 %collective-permute-start.4 = (bf16[16,384]{0,1:T(8,128)(2,1)S(1)}, bf16[16,384]{0,1:T(8,128)(2,1)S(1)}, u32[]{:S(2)}, u32[]{:S(2)}) collective-permute-start(bf16[16,384]{0,1:T(8,128)(2,1)S(1)} %copy.43), channel_id=1, source_target_pairs={{0,4},{1,5},{2,6},{3,7},{4,0},{5,1},{6,2},{7,3},{8,12},{9,13},{10,... | collective-permute-start | bytes 36872 | tf_op jit(solution)/shard_map/ppermute | solution.py:20
  16.9 1.3 %collective-permute-done.3 = bf16[16,384]{0,1:T(8,128)(2,1)S(1)} collective-permute-done((bf16[16,384]{0,1:T(8,128)(2,1)S(1)}, bf16[16,384]{0,1:T(8,128)(2,1)S(1)}, u32[]{:S(2)}, u32[]{:S(2)}) %collective-permute-start.3) | collective-permute-done | bytes 12320 | tf_op jit(solution)/shard_map/ppermute | solution.py:20
  18.2 1.2 %collective-permute-done.4 = bf16[16,384]{0,1:T(8,128)(2,1)S(1)} collective-permute-done((bf16[16,384]{0,1:T(8,128)(2,1)S(1)}, bf16[16,384]{0,1:T(8,128)(2,1)S(1)}, u32[]{:S(2)}, u32[]{:S(2)}) %collective-permute-start.4) | collective-permute-done | bytes 12320 | tf_op jit(solution)/shard_map/ppermute | solution.py:20
  19.5 1.8 %collective-permute-done.5 = bf16[16,384]{0,1:T(8,128)(2,1)S(1)} collective-permute-done((bf16[16,384]{0,1:T(8,128)(2,1)S(1)}, bf16[16,384]{0,1:T(8,128)(2,1)S(1)}, u32[]{:S(2)}, u32[]{:S(2)}) %collective-permute-start.5) | collective-permute-done | bytes 12320 | tf_op jit(solution)/shard_map/ppermute | solution.py:20
  21.6 1.2 %collective-permute-done.6 = bf16[64,384]{0,1:T(8,128)(2,1)S(1)} collective-permute-done((bf16[64,384]{0,1:T(8,128)(2,1)S(1)}, bf16[64,384]{0,1:T(8,128)(2,1)S(1)}, u32[]{:S(2)}, u32[]{:S(2)}) %collective-permute-start.6) | collective-permute-done | bytes 49184 | tf_op jit(solution)/shard_map/ppermute | solution.py:20
  23.7 8.1 %fusion.85 = (bf16[16,4096]{1,0:T(8,128)(2,1)S(1)}, f32[16,4096]{1,0:T(8,128)S(1)}) fusion(bf16[16,2048]{1,0:T(8,128)(2,1)S(1)} %reshape.141, bf16[2048,4096]{1,0:T(8,128)(2,1)} %param.15), kind=kOutput, calls=%fused_computation.158 | convolution fusion | flops 268500992 | bytes 17235968 | tf_op jit(solution)/shard_map/dot_general | solution.py:109
  32.1 5.3 %collective-permute-done.7 = bf16[16,4096]{1,0:T(8,128)(2,1)S(1)} collective-permute-done((bf16[16,4096]{1,0:T(8,128)(2,1)S(1)}, bf16[16,4096]{1,0:T(8,128)(2,1)S(1)}, u32[]{:S(2)}, u32[]{:S(2)}) %collective-permute-start.7) | collective-permute-done | bytes 131104 | tf_op jit(solution)/shard_map/ppermute | solution.py:20
  37.4 2.2 %collective-permute-start.8 = (bf16[16,4096]{1,0:T(8,128)(2,1)S(1)}, bf16[16,4096]{1,0:T(8,128)(2,1)S(1)}, u32[]{:S(2)}, u32[]{:S(2)}) collective-permute-start(bf16[16,4096]{1,0:T(8,128)(2,1)S(1)} %fusion.24), channel_id=1, source_target_pairs={{0,16},{8,24},{16,0},{24,8},{1,17},{9,25},{17,1},{25,9},{2,18},{10... | collective-permute-start | bytes 393224 | tf_op jit(solution)/shard_map/ppermute | solution.py:20
  39.5 6.3 %collective-permute-done.8 = bf16[16,4096]{1,0:T(8,128)(2,1)S(1)} collective-permute-done((bf16[16,4096]{1,0:T(8,128)(2,1)S(1)}, bf16[16,4096]{1,0:T(8,128)(2,1)S(1)}, u32[]{:S(2)}, u32[]{:S(2)}) %collective-permute-start.8) | collective-permute-done | bytes 131104 | tf_op jit(solution)/shard_map/ppermute | solution.py:20
  47.2 2.5 %collective-permute-start.11 = (bf16[16,4096]{1,0:T(8,128)(2,1)S(1)}, bf16[16,4096]{1,0:T(8,128)(2,1)S(1)}, u32[]{:S(2)}, u32[]{:S(2)}) collective-permute-start(bf16[16,4096]{1,0:T(8,128)(2,1)S(1)} %get-tuple-element.8), channel_id=1, source_target_pairs={{0,6},{1,7},{2,4},{3,5},{4,2},{5,3},{6,0},{7,1},{8,14},{9,15},{10,... | collective-permute-start | bytes 393224 | tf_op jit(solution)/shard_map/ppermute | solution.py:20
  49.8 2.8 %collective-permute-done.9 = bf16[16,4096]{1,0:T(8,128)(2,1)S(1)} collective-permute-done((bf16[16,4096]{1,0:T(8,128)(2,1)S(1)}, bf16[16,4096]{1,0:T(8,128)(2,1)S(1)}, u32[]{:S(2)}, u32[]{:S(2)}) %collective-permute-start.9) | collective-permute-done | bytes 131104 | tf_op jit(solution)/shard_map/ppermute | solution.py:20
  52.6 2.1 %collective-permute-done.10 = bf16[16,4096]{1,0:T(8,128)(2,1)S(1)} collective-permute-done((bf16[16,4096]{1,0:T(8,128)(2,1)S(1)}, bf16[16,4096]{1,0:T(8,128)(2,1)S(1)}, u32[]{:S(2)}, u32[]{:S(2)}) %collective-permute-start.10) | collective-permute-done | bytes 131104 | tf_op jit(solution)/shard_map/ppermute | solution.py:20
  54.9 1.8 %collective-permute-done.12 = bf16[64,4096]{1,0:T(8,128)(2,1)S(1)} collective-permute-done((bf16[64,4096]{1,0:T(8,128)(2,1)S(1)}, bf16[64,4096]{1,0:T(8,128)(2,1)S(1)}, u32[]{:S(2)}, u32[]{:S(2)}) %collective-permute-start.12) | collective-permute-done | bytes 524320 | tf_op jit(solution)/shard_map/ppermute | solution.py:20
  56.8 0.8 fusion
  57.5 3.1 %convolution_convert_fusion = bf16[80,512]{1,0:T(8,128)(2,1)S(1)} fusion(f32[128,512]{1,0:T(8,128)S(1)} %fusion, bf16[128,4096]{1,0:T(8,128)(2,1)S(1)} %constant_dynamic-update-slice_fusion.3, bf16[1,1,4096,512]{3,2,1,0:T(8,128)(2,1)} %param.19, s32[128]{0:T(128)S(1)} %get-tuple-element.44), kind=kOutput, calls=%fused_computation.15 | convolution fusion | flops 547801088 | bytes 5587456 | tf_op jit(solution)/shard_map/dot_general | solution.py:155
  60.6 1.2 %collective-permute-start.13 = (bf16[80,512]{1,0:T(8,128)(2,1)S(1)}, bf16[80,512]{1,0:T(8,128)(2,1)S(1)}, u32[]{:S(2)}, u32[]{:S(2)}) collective-permute-start(bf16[80,512]{1,0:T(8,128)(2,1)S(1)} %convolution_convert_fusion), channel_id=1, source_target_pairs={{0,24},{8,16},{16,8},{24,0},{1,25},{9,17},{17,9},{25,1},{2,26},{10... | collective-permute-start | bytes 245768 | tf_op jit(solution)/shard_map/ppermute | solution.py:20
  61.9 3.2 %collective-permute-start.15 = (bf16[80,512]{1,0:T(8,128)(2,1)S(1)}, bf16[80,512]{1,0:T(8,128)(2,1)S(1)}, u32[]{:S(2)}, u32[]{:S(2)}) collective-permute-start(bf16[80,512]{1,0:T(8,128)(2,1)S(1)} %convolution_convert_fusion), channel_id=1, source_target_pairs={{0,8},{8,0},{16,24},{24,16},{1,9},{9,1},{17,25},{25,17},{2,10},{10... | collective-permute-start | bytes 245768 | tf_op jit(solution)/shard_map/ppermute | solution.py:20
  65.2 2.7 %collective-permute-done.13 = bf16[80,512]{1,0:T(8,128)(2,1)S(1)} collective-permute-done((bf16[80,512]{1,0:T(8,128)(2,1)S(1)}, bf16[80,512]{1,0:T(8,128)(2,1)S(1)}, u32[]{:S(2)}, u32[]{:S(2)}) %collective-permute-start.13) | collective-permute-done | bytes 81952 | tf_op jit(solution)/shard_map/ppermute | solution.py:20
  67.9 2.6 %collective-permute-done.14 = bf16[80,512]{1,0:T(8,128)(2,1)S(1)} collective-permute-done((bf16[80,512]{1,0:T(8,128)(2,1)S(1)}, bf16[80,512]{1,0:T(8,128)(2,1)S(1)}, u32[]{:S(2)}, u32[]{:S(2)}) %collective-permute-start.14) | collective-permute-done | bytes 81952 | tf_op jit(solution)/shard_map/ppermute | solution.py:20
  70.5 2.1 %fusion.13 = bf16[80,1024]{1,0:T(8,128)(2,1)S(1)} fusion(bf16[2,1024,1024]{2,1,0:T(8,128)(2,1)} %param.21, bf16[80,512]{1,0:T(8,128)(2,1)S(1)} %get-tuple-element.18, bf16[80,512]{1,0:T(8,128)(2,1)S(1)} %get-tuple-element.17), kind=kOutput, calls=%fused_computation.11 | convolution fusion | flops 168181760 | bytes 2424832 | tf_op jit(solution)/shard_map/dot_general | solution.py:161
  72.6 2.1 %fusion.10 = bf16[80,1024]{1,0:T(8,128)(2,1)S(1)} fusion(bf16[2,1024,1024]{2,1,0:T(8,128)(2,1)} %param.21, bf16[80,512]{1,0:T(8,128)(2,1)S(1)} %get-tuple-element.16, bf16[80,512]{1,0:T(8,128)(2,1)S(1)} %get-tuple-element.15), kind=kOutput, calls=%fused_computation.10 | convolution fusion | flops 168181760 | bytes 2424832 | tf_op jit(solution)/shard_map/dot_general | solution.py:161
  75.2 1.3 %collective-permute-done.16 = bf16[64,1024]{1,0:T(8,128)(2,1)S(1)} collective-permute-done((bf16[64,1024]{1,0:T(8,128)(2,1)S(1)}, bf16[64,1024]{1,0:T(8,128)(2,1)S(1)}, u32[]{:S(2)}, u32[]{:S(2)}) %collective-permute-start.16) | collective-permute-done | bytes 131104 | tf_op jit(solution)/shard_map/ppermute | solution.py:20
  76.6 1.5 %collective-permute-start.19 = (bf16[16,1024]{1,0:T(8,128)(2,1)S(1)}, bf16[16,1024]{1,0:T(8,128)(2,1)S(1)}, u32[]{:S(2)}, u32[]{:S(2)}) collective-permute-start(bf16[16,1024]{1,0:T(8,128)(2,1)S(1)} %get-tuple-element.20), channel_id=1, source_target_pairs={{0,6},{1,7},{2,4},{3,5},{4,2},{5,3},{6,0},{7,1},{8,14},{9,15},{10,... | collective-permute-start | bytes 98312 | tf_op jit(solution)/shard_map/ppermute | solution.py:20
  78.1 1.5 %collective-permute-start.18 = (bf16[16,1024]{1,0:T(8,128)(2,1)S(1)}, bf16[16,1024]{1,0:T(8,128)(2,1)S(1)}, u32[]{:S(2)}, u32[]{:S(2)}) collective-permute-start(bf16[16,1024]{1,0:T(8,128)(2,1)S(1)} %get-tuple-element.21), channel_id=1, source_target_pairs={{0,4},{1,5},{2,6},{3,7},{4,0},{5,1},{6,2},{7,3},{8,12},{9,13},{10,... | collective-permute-start | bytes 98312 | tf_op jit(solution)/shard_map/ppermute | solution.py:20
  80.2 1.3 %collective-permute-done.19 = bf16[16,1024]{1,0:T(8,128)(2,1)S(1)} collective-permute-done((bf16[16,1024]{1,0:T(8,128)(2,1)S(1)}, bf16[16,1024]{1,0:T(8,128)(2,1)S(1)}, u32[]{:S(2)}, u32[]{:S(2)}) %collective-permute-start.19) | collective-permute-done | bytes 32800 | tf_op jit(solution)/shard_map/ppermute | solution.py:20
  82.1 1.5 %collective-permute-done.17 = bf16[16,1024]{1,0:T(8,128)(2,1)S(1)} collective-permute-done((bf16[16,1024]{1,0:T(8,128)(2,1)S(1)}, bf16[16,1024]{1,0:T(8,128)(2,1)S(1)}, u32[]{:S(2)}, u32[]{:S(2)}) %collective-permute-start.17) | collective-permute-done | bytes 32800 | tf_op jit(solution)/shard_map/ppermute | solution.py:20
  (73 shorter events, 9.5 us)
Async XLA Ops:
  2.6 7.7 %collective-permute-start = (bf16[4,2304]{1,0:T(4,128)(2,1)S(1)}, bf16[4,2304]{1,0:T(4,128)(2,1)S(1)}, u32[]{:S(2)}, u32[]{:S(2)}) collective-permute-start(bf16[4,2304]{1,0:T(4,128)(2,1)S(1)} %bitcast.55), channel_id=1, source_target_pairs={{0,24},{8,16},{16,8},{24,0},{1,25},{9,17},{17,9},{25,1},{2,26},{10... | collective-permute-start | bytes 55304 | tf_op jit(solution)/shard_map/ppermute | solution.py:20
  7.7 4.7 %collective-permute-start.1 = (bf16[4,2304]{1,0:T(4,128)(2,1)S(1)}, bf16[4,2304]{1,0:T(4,128)(2,1)S(1)}, u32[]{:S(2)}, u32[]{:S(2)}) collective-permute-start(bf16[4,2304]{1,0:T(4,128)(2,1)S(1)} %bitcast.56), channel_id=1, source_target_pairs={{0,16},{8,24},{16,0},{24,8},{1,17},{9,25},{17,1},{25,9},{2,18},{10... | collective-permute-start | bytes 55304 | tf_op jit(solution)/shard_map/ppermute | solution.py:20
  7.8 4.6 %collective-permute-start.2 = (bf16[4,2304]{1,0:T(4,128)(2,1)S(1)}, bf16[4,2304]{1,0:T(4,128)(2,1)S(1)}, u32[]{:S(2)}, u32[]{:S(2)}) collective-permute-start(bf16[4,2304]{1,0:T(4,128)(2,1)S(1)} %bitcast.57), channel_id=1, source_target_pairs={{0,8},{8,0},{16,24},{24,16},{1,9},{9,1},{17,25},{25,17},{2,10},{10... | collective-permute-start | bytes 55304 | tf_op jit(solution)/shard_map/ppermute | solution.py:20
  12.7 5.6 %collective-permute-start.3 = (bf16[16,384]{0,1:T(8,128)(2,1)S(1)}, bf16[16,384]{0,1:T(8,128)(2,1)S(1)}, u32[]{:S(2)}, u32[]{:S(2)}) collective-permute-start(bf16[16,384]{0,1:T(8,128)(2,1)S(1)} %copy.43), channel_id=1, source_target_pairs={{0,2},{1,3},{2,0},{3,1},{4,6},{5,7},{6,4},{7,5},{8,10},{9,11},{10,... | collective-permute-start | bytes 36872 | tf_op jit(solution)/shard_map/ppermute | solution.py:20
  14.2 5.2 %collective-permute-start.4 = (bf16[16,384]{0,1:T(8,128)(2,1)S(1)}, bf16[16,384]{0,1:T(8,128)(2,1)S(1)}, u32[]{:S(2)}, u32[]{:S(2)}) collective-permute-start(bf16[16,384]{0,1:T(8,128)(2,1)S(1)} %copy.43), channel_id=1, source_target_pairs={{0,4},{1,5},{2,6},{3,7},{4,0},{5,1},{6,2},{7,3},{8,12},{9,13},{10,... | collective-permute-start | bytes 36872 | tf_op jit(solution)/shard_map/ppermute | solution.py:20
  15.7 5.5 %collective-permute-start.5 = (bf16[16,384]{0,1:T(8,128)(2,1)S(1)}, bf16[16,384]{0,1:T(8,128)(2,1)S(1)}, u32[]{:S(2)}, u32[]{:S(2)}) collective-permute-start(bf16[16,384]{0,1:T(8,128)(2,1)S(1)} %copy.43), channel_id=1, source_target_pairs={{0,6},{1,7},{2,4},{3,5},{4,2},{5,3},{6,0},{7,1},{8,14},{9,15},{10,... | collective-permute-start | bytes 36872 | tf_op jit(solution)/shard_map/ppermute | solution.py:20
  21.4 1.4 %collective-permute-start.6 = (bf16[64,384]{0,1:T(8,128)(2,1)S(1)}, bf16[64,384]{0,1:T(8,128)(2,1)S(1)}, u32[]{:S(2)}, u32[]{:S(2)}) collective-permute-start(bf16[64,384]{0,1:T(8,128)(2,1)S(1)} %pad_maximum_fusion.1), channel_id=1, source_target_pairs={{0,1},{1,0},{2,3},{3,2},{4,5},{5,4},{6,7},{7,6},{8,9},{9,8},{10,11... | collective-permute-start | bytes 147464 | tf_op jit(solution)/shard_map/ppermute | solution.py:20
  23.7 22.2 %copy-start.1 = (bf16[1,16,4096]{2,1,0:T(8,128)(2,1)S(1)}, bf16[1,16,4096]{2,1,0:T(8,128)(2,1)}, u32[]{:S(2)}) copy-start(bf16[1,16,4096]{2,1,0:T(8,128)(2,1)} %param.14) | copy-start | bytes 393220
  31.8 25.0 %copy-start = (bf16[1,1,4096,512]{3,2,1,0:T(8,128)(2,1)S(1)}, bf16[1,1,4096,512]{3,2,1,0:T(8,128)(2,1)}, u32[]{:S(2)}) copy-start(bf16[1,1,4096,512]{3,2,1,0:T(8,128)(2,1)} %param.20) | copy-start | bytes 12582916
  31.8 5.6 %collective-permute-start.7 = (bf16[16,4096]{1,0:T(8,128)(2,1)S(1)}, bf16[16,4096]{1,0:T(8,128)(2,1)S(1)}, u32[]{:S(2)}, u32[]{:S(2)}) collective-permute-start(bf16[16,4096]{1,0:T(8,128)(2,1)S(1)} %get-tuple-element.42), channel_id=1, source_target_pairs={{0,8},{8,0},{16,24},{24,16},{1,9},{9,1},{17,25},{25,17},{2,10},{10... | collective-permute-start | bytes 393224 | tf_op jit(solution)/shard_map/ppermute | solution.py:20
  37.4 8.5 %collective-permute-start.8 = (bf16[16,4096]{1,0:T(8,128)(2,1)S(1)}, bf16[16,4096]{1,0:T(8,128)(2,1)S(1)}, u32[]{:S(2)}, u32[]{:S(2)}) collective-permute-start(bf16[16,4096]{1,0:T(8,128)(2,1)S(1)} %fusion.24), channel_id=1, source_target_pairs={{0,16},{8,24},{16,0},{24,8},{1,17},{9,25},{17,1},{25,9},{2,18},{10... | collective-permute-start | bytes 393224 | tf_op jit(solution)/shard_map/ppermute | solution.py:20
  46.1 6.4 %collective-permute-start.9 = (bf16[16,4096]{1,0:T(8,128)(2,1)S(1)}, bf16[16,4096]{1,0:T(8,128)(2,1)S(1)}, u32[]{:S(2)}, u32[]{:S(2)}) collective-permute-start(bf16[16,4096]{1,0:T(8,128)(2,1)S(1)} %get-tuple-element.8), channel_id=1, source_target_pairs={{0,2},{1,3},{2,0},{3,1},{4,6},{5,7},{6,4},{7,5},{8,10},{9,11},{10,... | collective-permute-start | bytes 393224 | tf_op jit(solution)/shard_map/ppermute | solution.py:20
  46.7 7.9 %collective-permute-start.10 = (bf16[16,4096]{1,0:T(8,128)(2,1)S(1)}, bf16[16,4096]{1,0:T(8,128)(2,1)S(1)}, u32[]{:S(2)}, u32[]{:S(2)}) collective-permute-start(bf16[16,4096]{1,0:T(8,128)(2,1)S(1)} %get-tuple-element.8), channel_id=1, source_target_pairs={{0,4},{1,5},{2,6},{3,7},{4,0},{5,1},{6,2},{7,3},{8,12},{9,13},{10,... | collective-permute-start | bytes 393224 | tf_op jit(solution)/shard_map/ppermute | solution.py:20
  47.2 7.4 %collective-permute-start.11 = (bf16[16,4096]{1,0:T(8,128)(2,1)S(1)}, bf16[16,4096]{1,0:T(8,128)(2,1)S(1)}, u32[]{:S(2)}, u32[]{:S(2)}) collective-permute-start(bf16[16,4096]{1,0:T(8,128)(2,1)S(1)} %get-tuple-element.8), channel_id=1, source_target_pairs={{0,6},{1,7},{2,4},{3,5},{4,2},{5,3},{6,0},{7,1},{8,14},{9,15},{10,... | collective-permute-start | bytes 393224 | tf_op jit(solution)/shard_map/ppermute | solution.py:20
  54.7 2.0 %collective-permute-start.12 = (bf16[64,4096]{1,0:T(8,128)(2,1)S(1)}, bf16[64,4096]{1,0:T(8,128)(2,1)S(1)}, u32[]{:S(2)}, u32[]{:S(2)}) collective-permute-start(bf16[64,4096]{1,0:T(8,128)(2,1)S(1)} %pad_maximum_fusion), channel_id=1, source_target_pairs={{0,1},{1,0},{2,3},{3,2},{4,5},{5,4},{6,7},{7,6},{8,9},{9,8},{10,11... | collective-permute-start | bytes 1572872 | tf_op jit(solution)/shard_map/ppermute | solution.py:20
  60.6 7.3 %collective-permute-start.13 = (bf16[80,512]{1,0:T(8,128)(2,1)S(1)}, bf16[80,512]{1,0:T(8,128)(2,1)S(1)}, u32[]{:S(2)}, u32[]{:S(2)}) collective-permute-start(bf16[80,512]{1,0:T(8,128)(2,1)S(1)} %convolution_convert_fusion), channel_id=1, source_target_pairs={{0,24},{8,16},{16,8},{24,0},{1,25},{9,17},{17,9},{25,1},{2,26},{10... | collective-permute-start | bytes 245768 | tf_op jit(solution)/shard_map/ppermute | solution.py:20
  61.9 8.6 %collective-permute-start.14 = (bf16[80,512]{1,0:T(8,128)(2,1)S(1)}, bf16[80,512]{1,0:T(8,128)(2,1)S(1)}, u32[]{:S(2)}, u32[]{:S(2)}) collective-permute-start(bf16[80,512]{1,0:T(8,128)(2,1)S(1)} %convolution_convert_fusion), channel_id=1, source_target_pairs={{0,16},{8,24},{16,0},{24,8},{1,17},{9,25},{17,1},{25,9},{2,18},{10... | collective-permute-start | bytes 245768 | tf_op jit(solution)/shard_map/ppermute | solution.py:20
  61.9 8.6 %collective-permute-start.15 = (bf16[80,512]{1,0:T(8,128)(2,1)S(1)}, bf16[80,512]{1,0:T(8,128)(2,1)S(1)}, u32[]{:S(2)}, u32[]{:S(2)}) collective-permute-start(bf16[80,512]{1,0:T(8,128)(2,1)S(1)} %convolution_convert_fusion), channel_id=1, source_target_pairs={{0,8},{8,0},{16,24},{24,16},{1,9},{9,1},{17,25},{25,17},{2,10},{10... | collective-permute-start | bytes 245768 | tf_op jit(solution)/shard_map/ppermute | solution.py:20
  75.1 1.4 %collective-permute-start.16 = (bf16[64,1024]{1,0:T(8,128)(2,1)S(1)}, bf16[64,1024]{1,0:T(8,128)(2,1)S(1)}, u32[]{:S(2)}, u32[]{:S(2)}) collective-permute-start(bf16[64,1024]{1,0:T(8,128)(2,1)S(1)} %slice.131), channel_id=1, source_target_pairs={{0,1},{1,0},{2,3},{3,2},{4,5},{5,4},{6,7},{7,6},{8,9},{9,8},{10,11... | collective-permute-start | bytes 393224 | tf_op jit(solution)/shard_map/ppermute | solution.py:20
  76.6 4.9 %collective-permute-start.19 = (bf16[16,1024]{1,0:T(8,128)(2,1)S(1)}, bf16[16,1024]{1,0:T(8,128)(2,1)S(1)}, u32[]{:S(2)}, u32[]{:S(2)}) collective-permute-start(bf16[16,1024]{1,0:T(8,128)(2,1)S(1)} %get-tuple-element.20), channel_id=1, source_target_pairs={{0,6},{1,7},{2,4},{3,5},{4,2},{5,3},{6,0},{7,1},{8,14},{9,15},{10,... | collective-permute-start | bytes 98312 | tf_op jit(solution)/shard_map/ppermute | solution.py:20
  78.1 3.9 %collective-permute-start.18 = (bf16[16,1024]{1,0:T(8,128)(2,1)S(1)}, bf16[16,1024]{1,0:T(8,128)(2,1)S(1)}, u32[]{:S(2)}, u32[]{:S(2)}) collective-permute-start(bf16[16,1024]{1,0:T(8,128)(2,1)S(1)} %get-tuple-element.21), channel_id=1, source_target_pairs={{0,4},{1,5},{2,6},{3,7},{4,0},{5,1},{6,2},{7,3},{8,12},{9,13},{10,... | collective-permute-start | bytes 98312 | tf_op jit(solution)/shard_map/ppermute | solution.py:20
  79.7 3.9 %collective-permute-start.17 = (bf16[16,1024]{1,0:T(8,128)(2,1)S(1)}, bf16[16,1024]{1,0:T(8,128)(2,1)S(1)}, u32[]{:S(2)}, u32[]{:S(2)}) collective-permute-start(bf16[16,1024]{1,0:T(8,128)(2,1)S(1)} %get-tuple-element.19), channel_id=1, source_target_pairs={{0,2},{1,3},{2,0},{3,1},{4,6},{5,7},{6,4},{7,5},{8,10},{9,11},{10,... | collective-permute-start | bytes 98312 | tf_op jit(solution)/shard_map/ppermute | solution.py:20

commit v2 on v1

--- a/solution.py
+++ b/solution.py
@@ -1,6 +1,8 @@
 import jax
 import jax.numpy as jnp
 from jax import lax
+from jax.experimental import pallas as pl
+from jax.experimental.pallas import tpu as pltpu
 from jax.sharding import PartitionSpec as P
 
 D = 4096
@@ -14,6 +16,138 @@
 
 norm_eps = 1e-06
 masked_score = -1e30
+
+
+def fetch(sources, after, cuts=1):
+    shapes = [(source.shape[0] // cuts,) + source.shape[1:] for source in sources for _ in range(cuts)]
+
+    def body(*refs):
+        n = len(sources)
+        copies = []
+        for i, shape in enumerate(shapes):
+            source = refs[i // cuts].at[pl.ds(i % cuts * shape[0], shape[0])]
+            target, sem = refs[n + 1 + i], refs[n + 1 + n * cuts].at[i]
+            copies.append(pltpu.make_async_copy(source, target, sem))
+        for copy in copies:
+            copy.start()
+        for copy in copies:
+            copy.wait()
+
+    moved = sum(source.size * source.dtype.itemsize for source in sources)
+    return pl.pallas_call(
+        body,
+        out_shape=[pltpu.VMEM(shape, sources[0].dtype) for shape in shapes],
+        in_specs=[pl.BlockSpec(memory_space=pltpu.HBM)] * len(sources)
+        + [pl.BlockSpec(memory_space=pl.ANY)],
+        out_specs=[pl.BlockSpec(memory_space=pltpu.VMEM)] * len(shapes),
+        scratch_shapes=[pltpu.SemaphoreType.DMA((len(shapes),))],
+        compiler_params=pltpu.CompilerParams(vmem_limit_bytes=1 << 20),
+        cost_estimate=pl.CostEstimate(flops=0, transcendentals=0, bytes_accessed=2 * moved),
+    )(*[in_hbm(source) for source in sources], after)
+
+
+def in_hbm(array):
+    return pltpu.with_memory_space_constraint(array, pltpu.HBM)
+
+
+def in_vmem(array):
+    return pltpu.with_memory_space_constraint(array, pltpu.VMEM)
+
+
+def local_call(body, outs, *operands, flops=0, scratch=(), streamed=(), limit=8 << 20):
+    moved = sum(a.size * a.dtype.itemsize for a in operands + tuple(streamed))
+    spec = pl.BlockSpec(memory_space=pltpu.VMEM)
+    return pl.pallas_call(
+        body,
+        out_shape=[pltpu.VMEM(shape, dtype) for shape, dtype in outs],
+        in_specs=[spec] * len(operands)
+        + [pl.BlockSpec(memory_space=pltpu.HBM)] * len(streamed),
+        out_specs=[spec] * len(outs),
+        scratch_shapes=list(scratch),
+        compiler_params=pltpu.CompilerParams(vmem_limit_bytes=limit),
+        cost_estimate=pl.CostEstimate(flops=flops, transcendentals=0, bytes_accessed=moved),
+    )(*[in_vmem(a) for a in operands], *[in_hbm(a) for a in streamed])
+
+
+def column_tile(width):
+    return next(tile for tile in (512, 256, 128, width) if width % tile == 0)
+
+
+def attend_body(rows_ref, pairs_ref, *refs):
+    weight_hbm, wide_ref, sent_ref, held_ref, weight_ref, sems = refs
+    width = wide_ref.shape[1]
+    tile = column_tile(width)
+    copies = []
+    for i in range(width // tile):
+        cols = pl.ds(i * tile, tile)
+        copies.append(
+            pltpu.make_async_copy(weight_hbm.at[:, cols], weight_ref.at[:, cols], sems.at[i])
+        )
+        copies[i].start()
+    column = rows_ref.shape[0]
+    heads = rows_ref.shape[1] // HEAD_DIM
+    seq_count, exp_count, e = lax.axis_size("seq"), lax.axis_size("exp"), lax.axis_index("exp")
+    tok_dev = column // seq_count
+    q = jnp.concatenate(
+        [rows_ref[:, h * HEAD_DIM : (h + 1) * HEAD_DIM] for h in range(heads)], axis=0
+    )
+    keys = pairs_ref[:, :HEAD_DIM]
+    vals = pairs_ref[:, HEAD_DIM : 2 * HEAD_DIM]
+    scores = lax.dot_general(
+        q, keys, (((1,), (1,)), ((), ())), preferred_element_type=jnp.float32
+    ) * (HEAD_DIM ** (-0.5))
+    row = lax.broadcasted_iota(jnp.int32, scores.shape, 1)
+    key_pos = gathered_pos(row, tok_dev, exp_count, column)
+    query_pos = e * column + lax.broadcasted_iota(jnp.int32, scores.shape, 0) % column
+    allowed = key_pos <= query_pos
+    scores = jnp.where(allowed, scores, masked_score)
+    top = jnp.max(scores, axis=1, keepdims=True)
+    weights_of = jnp.where(allowed, jnp.exp(scores - top), 0.0)
+    total = jnp.sum(weights_of, axis=1, keepdims=True)
+    mixed = jnp.dot(weights_of.astype(jnp.bfloat16), vals, preferred_element_type=jnp.float32)
+    mixed = (mixed / total).astype(jnp.bfloat16)
+    for h in range(heads):
+        held_ref[:, h * HEAD_DIM : (h + 1) * HEAD_DIM] = mixed[h * column : (h + 1) * column]
+    for i, copy in enumerate(copies):
+        copy.wait()
+        cols = pl.ds(i * tile, tile)
+        out = jnp.dot(held_ref[...], weight_ref[:, cols], preferred_element_type=jnp.float32)
+        wide_ref[:, cols] = out
+        sent_ref[:, cols] = out.astype(sent_ref.dtype)
+
+
+def gathered_pos(row, tok_dev, exp_count, column):
+    group = row // tok_dev
+    return group % exp_count * column + group // exp_count * tok_dev + row % tok_dev
+
+
+def units_body(rows_ref, gate_ref, up_ref, out_ref):
+    width = gate_ref.shape[1]
+    tile = min(256, column_tile(width))
+
+    def step(i, carry):
+        cols = pl.ds(pl.multiple_of(i * tile, tile), tile)
+        gate = jnp.dot(rows_ref[...], gate_ref[:, cols], preferred_element_type=jnp.float32)
+        up = jnp.dot(rows_ref[...], up_ref[:, cols], preferred_element_type=jnp.float32)
+        out_ref[:, cols] = (gate / (1.0 + jnp.exp(-gate)) * up).astype(out_ref.dtype)
+        return carry
+
+    lax.fori_loop(0, width // tile, step, 0)
+
+
+def down_body(rows_ref, weight_ref, out_ref):
+    count, _, width = weight_ref.shape
+    tile = min(256, column_tile(width))
+
+    def step(i, carry):
+        cols = pl.ds(pl.multiple_of(i * tile, tile), tile)
+        for p in range(count):
+            out = jnp.dot(rows_ref[p], weight_ref[p, :, cols], preferred_element_type=jnp.float32)
+            out_ref[p, :, cols] = out.astype(out_ref.dtype)
+        return carry
+
+    lax.fori_loop(0, width // tile, step, 0)
+
 
 def exchange(value, axis, step):
     count = lax.axis_size(axis)
@@ -52,64 +186,70 @@
     head_dev = HEADS // seq_count
     exp_dev = down_weight.shape[0]
     experts = exp_dev * exp_count
-    steps = list(range(0, exp_count, 2)) + list(range(1, exp_count, 2))
     half = exp_count // 2
     tokens = exp_count * column
 
-    q_local = queries.reshape(tok_dev, seq_count, head_dev * HEAD_DIM)
-    k_local = key_rows.reshape(tok_dev, KV_HEADS, HEAD_DIM)
-    v_local = values.reshape(tok_dev, KV_HEADS, HEAD_DIM)
-    reps = seq_count // KV_HEADS
-    wide = jnp.concatenate(
-        [q_local, jnp.repeat(k_local, reps, axis=1), jnp.repeat(v_local, reps, axis=1)], axis=2
-    )
+    width = head_dev * HEAD_DIM
+    q_rows = queries[0]
     pieces = []
     for k in range(seq_count):
-        piece = lax.dynamic_index_in_dim(wide, s ^ k, 1, keepdims=False)
+        piece = lax.dynamic_slice_in_dim(q_rows, (s ^ k) * width, width, 1)
         pieces.append(piece if k == 0 else exchange(piece, "seq", k))
-    rows = jnp.concatenate(in_order(pieces, s), axis=0)
-    q_heads = rows[:, : head_dev * HEAD_DIM].reshape(column * head_dev, HEAD_DIM)
 
     expert_of = lax.iota(jnp.int32, experts)
+    own_ids = lax.dynamic_slice_in_dim(expert_ids[0], s * tok_dev, tok_dev, 0)
+    own_weights = lax.dynamic_slice_in_dim(route_weights[0], s * tok_dev, tok_dev, 0)
     table = jnp.sum(
-        jnp.where(
-            expert_ids[0][:, :, None] == expert_of[None, None, :], route_weights[0][:, :, None], 0.0
-        ),
+        jnp.where(own_ids[:, :, None] == expert_of[None, None, :], own_weights[:, :, None], 0.0),
         axis=1,
     )
     high = lax.reduce_precision(table, 8, 7)
     middle = lax.reduce_precision(table - high, 8, 7)
     low = table - high - middle
-    lanes = 128
     packed = jnp.concatenate([high, middle, low], axis=1).astype(bf16)
-    packed = jnp.pad(packed, ((0, 0), (0, -packed.shape[1] % lanes)))
-    block = jnp.concatenate([rows[:, head_dev * HEAD_DIM :], packed], axis=1)
-    near = jnp.concatenate(
-        [block] + [exchange(block, "exp", k) for k in range(2, exp_count, 2)], axis=0
-    )
-    gathered = jnp.concatenate([near, exchange(near, "exp", 1)], axis=0)
-    keys = gathered[:, :HEAD_DIM]
-    vals = gathered[:, HEAD_DIM : 2 * HEAD_DIM]
-    terms = gathered[:, 2 * HEAD_DIM : 2 * HEAD_DIM + 3 * experts].astype(f32)
-    weight_of = terms[:, :experts] + terms[:, experts : 2 * experts] + terms[:, 2 * experts :]
-
-    position = lax.iota(jnp.int32, tokens)
+    packed = jnp.pad(packed, ((0, 0), (0, -packed.shape[1] % 128)))
+
+    reps = seq_count // KV_HEADS
+    parts = []
+    for j in range(seq_count):
+        cut = slice(j // reps * HEAD_DIM, (j // reps + 1) * HEAD_DIM)
+        parts.append(jnp.concatenate([key_rows[0][:, cut], values[0][:, cut], packed], axis=1))
+    parts = jnp.stack(parts, axis=0)
+    parts = jnp.broadcast_to(parts[:, None], (seq_count, exp_count) + parts.shape[1:])
+    parts = parts.reshape((seq_count * exp_count,) + parts.shape[2:])
+    gathered = lax.all_to_all(parts, ("seq", "exp"), split_axis=0, concat_axis=0, tiled=True)
+    gathered = gathered.reshape(tokens, gathered.shape[2])
+    rows = jnp.concatenate(in_order(pieces, s), axis=0)
+    row = lax.iota(jnp.int32, tokens)
+    key_pos = gathered_pos(row, tok_dev, exp_count, column)
+    position = row
     step_of = position // column
     step_of = jnp.where(step_of < half, 2 * step_of, 2 * (step_of - half) + 1)
-    key_pos = (e ^ step_of) * column + position % column
-    query_pos = e * column + lax.iota(jnp.int32, column * head_dev) // head_dev
-    scores = jnp.dot(q_heads, keys.T, preferred_element_type=f32) * (HEAD_DIM ** (-0.5))
-    allowed = key_pos[None, :] <= query_pos[:, None]
-    scores = jnp.where(allowed, scores, masked_score)
-    top = jnp.max(scores, axis=1, keepdims=True)
-    weights = jnp.where(allowed, jnp.exp(scores - top), 0.0)
-    total = jnp.sum(weights, axis=1, keepdims=True)
-    attended = jnp.dot(weights.astype(bf16), vals, preferred_element_type=f32) / total
-    attended = attended.astype(bf16).reshape(column, head_dev * HEAD_DIM)
-    projected = jnp.dot(attended, out_proj, preferred_element_type=f32)
+    place = (e ^ step_of) * column + position % column
+    reorder = (place[:, None] == key_pos[None, :]).astype(bf16)
+    terms = jnp.dot(reorder, gathered[:, 2 * HEAD_DIM :], preferred_element_type=f32)
+    weight_of = (
+        terms[:, :experts] + terms[:, experts : 2 * experts] + terms[:, 2 * experts : 3 * experts]
+    )
+
+    projected, sent = local_call(
+        attend_body,
+        [((column, D), f32), ((column, D), bf16)],
+        rows,
+        gathered[:, : 2 * HEAD_DIM],
+        flops=2 * column * out_proj.size,
+        scratch=[
+            pltpu.VMEM((column, width), bf16),
+            pltpu.VMEM(out_proj.shape, bf16),
+            pltpu.SemaphoreType.DMA((D // column_tile(D),)),
+        ],
+        streamed=[out_proj],
+        limit=24 << 20,
+    )
     step = 1
     while step < seq_count:
-        projected = projected + exchange(projected.astype(bf16), "seq", step).astype(f32)
+        projected = projected + exchange(sent, "seq", step).astype(f32)
+        sent = projected.astype(bf16)
         step *= 2
     hidden_one = residual[0].astype(f32) + projected
     mean_square = jnp.mean(hidden_one * hidden_one, axis=1, keepdims=True)
@@ -139,34 +279,38 @@
         axis=1,
     )
 
-    near = jnp.concatenate(
-        [normed] + [exchange(normed, "exp", k) for k in range(2, exp_count, 2)], axis=0
-    )
+    near = [normed] + [exchange(normed, "exp", k) for k in range(2, exp_count, 2)]
+    gate_local, up_local = fetch([gate_weight[0, 0], up_weight[0, 0]], normed)
+    near = jnp.concatenate(near, axis=0)
     far = exchange(near, "exp", 1)
-    gate_local = gate_weight[0, 0]
-    up_local = up_weight[0, 0]
 
     def units(part):
-        gate_vals = jnp.dot(part, gate_local, preferred_element_type=f32)
-        up_vals = jnp.dot(part, up_local, preferred_element_type=f32)
-        return (jax.nn.silu(gate_vals) * up_vals).astype(bf16)
-
-    activated = units(jnp.concatenate([near, far], axis=0))
+        return local_call(
+            units_body,
+            [((part.shape[0], gate_local.shape[1]), bf16)],
+            part,
+            gate_local,
+            up_local,
+            flops=4 * part.shape[0] * gate_local.size,
+        )[0]
+
+    activated = jnp.concatenate([units(near), units(far)], axis=0)
     activated = jnp.dot(pick, activated, preferred_element_type=f32).astype(bf16)
     pieces = [activated] + [exchange(activated, "seq", k) for k in range(1, seq_count)]
+    (down_local,) = fetch([down_weight], activated)
     pieces = in_order(pieces, s)
     group = seq_count // exp_dev
-    outputs = jnp.concatenate(
-        [
-            jnp.dot(
-                jnp.concatenate(pieces[p * group : (p + 1) * group], axis=1),
-                down_weight[p],
-                preferred_element_type=f32,
-            )
-            for p in range(exp_dev)
-        ],
-        axis=0,
-    ).astype(bf16)
+    rows_in = jnp.stack(
+        [jnp.concatenate(pieces[p * group : (p + 1) * group], axis=1) for p in range(exp_dev)], axis=0
+    )
+    (outputs,) = local_call(
+        down_body,
+        [((exp_dev, slots, col_width), bf16)],
+        rows_in,
+        down_local,
+        flops=2 * slots * down_weight.size,
+    )
+    outputs = outputs.reshape(exp_dev * slots, col_width)
     routed = jnp.dot(
         combine, outputs.astype(f32), precision=lax.Precision.HIGHEST, preferred_element_type=f32
     )
@@ -260,9 +404,7 @@
     def unchanged(current):
         return current
 
-    top_score, weight_sum, accumulated = lax.cond(
-        jnp.int32(0) <= last_query, update, unchanged, starting
-    )
+    _, weight_sum, accumulated = lax.cond(jnp.int32(0) <= last_query, update, unchanged, starting)
     attended = (accumulated / weight_sum[:, :, None]).astype(jnp.bfloat16)
     projected = jnp.einsum(
         "hqd,hde->qe",
@@ -341,4 +483,6 @@
         P("exp", None, "seq"),
     )
     out_specs = P("exp", None, "seq")
-    return jax.shard_map(shards, mesh=mesh, in_specs=in_specs, out_specs=out_specs, check_vma=False)
+    return jax.shard_map(
+        shards, mesh=mesh, in_specs=in_specs, out_specs=out_specs, check_vma=False
+    )

time: 84.6 us -> 76.8 us (0.908)
  Pallas kernels: 0 us -> 17.1 us
  matrix products: 17.3 us -> 1.04 us
  waiting for transfers between devices: 36 us -> 24.1 us
  starting transfers between devices: 23.3 us -> 26 us
  other arithmetic: 2.58 us -> 3.78 us
    pallas_call x0 -> x6, Pallas kernels: none -> 17.1 us  [the longest x4 11.4 us: local_call(): pl.pallas_call(body, out_shape=[pltpu.VMEM(shape, dtype) for shape, dtype...]
    dot_general x6 -> x1, matrix products: 13.5 us -> 0.24 us  [compact(): jnp.dot(reorder, gathered[:, 2 * HEAD_DIM:], preferred_element_type=f32)]
    ppermute x20 -> x16, waiting for transfers between devices: 36 us -> 24.1 us  [exchange(): return lax.ppermute(value, axis, [(i, i ^ step) for i in range(count)])]
    all_to_all x0 -> x1, starting transfers between devices: none -> 7.33 us  [compact(): lax.all_to_all(parts, ('seq', 'exp'), split_axis=0, concat_axis=0, tiled=...]
    ppermute x20 -> x16, starting transfers between devices: 23.3 us -> 18.6 us  [exchange(): return lax.ppermute(value, axis, [(i, i ^ step) for i in range(count)])]
    dot_general x1, matrix products: 3.1 us -> 0.16 us  [compact(): jnp.dot(pick, activated, preferred_element_type=f32).astype(bf16)]
    dynamic_slice x1 -> x5, local copies, waits for them, and re-layouts: 0.16 us -> 1.78 us  [the longest x2 0.84 us: compact(): lax.dynamic_slice_in_dim(route_weights[0], s * tok_dev, tok_dev, 0)]
    another operation x2 -> x0, local copies, waits for them, and re-layouts: 1.39 us -> none  [the longest x1 0.7 us: compact(): jnp.repeat(k_local, reps, axis=1)]
  transfers between devices with their start and end apart: 20 -> 17, of which waited for: 16 -> 12; matrix products, arithmetic and copies ran while one was open for 4% -> 4% of each run, Pallas kernels for 0% -> 10%
where the time goes in v2:
time: 76.8 us; the launch traced here: 76.2 us
  starting transfers between devices  26 us (34%)
  waiting for transfers between devices  24.1 us (31%)
  Pallas kernels  17.1 us (22%)
  local copies, waits for them, and re-layouts  3.93 us (5%)
  other arithmetic  3.78 us (5%)
  matrix products  1.04 us (1%)
    ppermute x16, waiting for transfers between devices, exchange(): return lax.ppermute(value, axis, [(i, i ^ step) for i in range(count)])  24.1 us
    ppermute x16, starting transfers between devices, exchange(): return lax.ppermute(value, axis, [(i, i ^ step) for i in range(count)])  18.6 us
    pallas_call x4, Pallas kernels, local_call(): pl.pallas_call(body, out_shape=[pltpu.VMEM(shape, dtype) for shape, dtype...  11.4 us
    all_to_all x1, starting transfers between devices, compact(): lax.all_to_all(parts, ('seq', 'exp'), split_axis=0, concat_axis=0, tiled=...  7.33 us
    pallas_call x2, Pallas kernels, fetch(): pl.pallas_call(body, out_shape=[pltpu.VMEM(shape, sources[0].dtype) for s...  5.69 us
  transfers between devices with their start and end apart: 17, of which 12 were waited for; matrix products, arithmetic and copies ran while one was open for 4% of the time, Pallas kernels for 10%

profile of v2, /device:TPU:0, one launch (start us, length us, event | category | flops | bytes accessed | tf_op | source)
XLA Modules:
  0.0 76.2 jit_solution(9499000036604150335)
XLA Ops:
  0.0 0.7 copy-done
  0.8 0.8 constant_dynamic-slice_fusion.3
  1.8 0.7 fusion.54
  2.5 0.8 %fusion.53 = (bf16[4,128]{1,0:T(4,128)(2,1)S(1)}, bf16[4,128]{1,0:T(4,128)(2,1)S(1)}, bf16[4,128]{1,0:T(4,128)(2,1)S(1)}, bf16[4,128]{1,0:T(4,128)(2,1)S(1)}, bf16[4,128]{1,0:T(4,128)(2,1)S(1)}) fusion(bf16[4,512]{1,0:T(4,128)(2,1)} %bitcast.57, bf16[4,16]{1,0:T(4,128)(2,1)S(1)} %get-tuple-element.43, bf16[4,16]{1,0:T(4,128)(2,1)S(1)} %get-tuple-element.44, ...), kind=kLoop, calls=%fused_computation.129 | loop fusion | flops 5120 | bytes 9600 | tf_op jit(solution)/shard_map/slice | solution.py:216
  4.0 7.3 %all-to-all-start = ((bf16[32,4,384]{2,1,0:T(4,128)(2,1)}), bf16[32,4,384]{2,1,0:T(4,128)(2,1)S(1)}, u32[]{:S(2)}, u32[]{:S(2)}) async-start(bf16[32,4,384]{2,1,0:T(4,128)(2,1)} %bitcast.13), calls=%async_computation | async-start | bytes 196608 | tf_op jit(solution)/shard_map/all_to_all | solution.py:220
  11.4 0.8 %dynamic-slice_bitcast_fusion = (bf16[4,2048]{1,0:T(4,128)(2,1)S(1)}, bf16[4,2048]{1,0:T(4,128)(2,1)S(1)}, bf16[4,2048]{1,0:T(4,128)(2,1)S(1)}) fusion(bf16[1,4,8192]{2,1,0:T(4,128)(2,1)} %param.11, s32[]{:T(128)S(6)} %select_n.206, s32[]{:T(128)S(6)} %select_n.204, s32[]{:T(128)S(6)} %select_n.203), kind=kLoop, calls=%fused_computation.57 | loop fusion | bytes 98316 | tf_op jit(solution)/shard_map/dynamic_slice | solution.py:196
  12.2 3.7 %collective-permute-start = (bf16[4,2048]{1,0:T(4,128)(2,1)S(1)}, bf16[4,2048]{1,0:T(4,128)(2,1)S(1)}, u32[]{:S(2)}, u32[]{:S(2)}) collective-permute-start(bf16[4,2048]{1,0:T(4,128)(2,1)S(1)} %get-tuple-element.33), channel_id=1, source_target_pairs={{0,24},{8,16},{16,8},{24,0},{1,25},{9,17},{17,9},{25,1},{2,26},{10... | collective-permute-start | bytes 49160 | tf_op jit(solution)/shard_map/ppermute | solution.py:154
  15.8 0.8 %collective-permute-start.2 = (bf16[4,2048]{1,0:T(4,128)(2,1)S(1)}, bf16[4,2048]{1,0:T(4,128)(2,1)S(1)}, u32[]{:S(2)}, u32[]{:S(2)}) collective-permute-start(bf16[4,2048]{1,0:T(4,128)(2,1)S(1)} %get-tuple-element.31), channel_id=1, source_target_pairs={{0,8},{8,0},{16,24},{24,16},{1,9},{9,1},{17,25},{25,17},{2,10},{10... | collective-permute-start | bytes 49160 | tf_op jit(solution)/shard_map/ppermute | solution.py:154
  16.7 0.7 convert_element_type.60
  18.0 2.5 %collective-permute-done.1 = bf16[4,2048]{1,0:T(4,128)(2,1)S(1)} collective-permute-done((bf16[4,2048]{1,0:T(4,128)(2,1)S(1)}, bf16[4,2048]{1,0:T(4,128)(2,1)S(1)}, u32[]{:S(2)}, u32[]{:S(2)}) %collective-permute-start.1) | collective-permute-done | bytes 16416 | tf_op jit(solution)/shard_map/ppermute | solution.py:154
  20.5 0.8 broadcast_select_fusion.13
  21.4 6.6 %shard_map.109 = (f32[16,4096]{1,0:T(8,128)S(1)}, bf16[16,4096]{1,0:T(8,128)(2,1)S(1)}) custom-call(bf16[16,2048]{1,0:T(8,128)(2,1)S(1)} %pad_maximum_fusion.2.rows_ref, bf16[128,256]{1,0:T(8,128)(2,1)S(1)} %slice.104.pairs_ref, bf16[2048,4096]{1,0:T(8,128)(2,1)} %refs_0_.2), custom_call_target="tpu_custom_call" | custom-call | flops 268435456 | bytes 16908288 | tf_op jit(solution)/shard_map/pallas_call | solution.py:60
  28.3 4.7 %collective-permute-done.3 = bf16[16,4096]{1,0:T(8,128)(2,1)S(1)} collective-permute-done((bf16[16,4096]{1,0:T(8,128)(2,1)S(1)}, bf16[16,4096]{1,0:T(8,128)(2,1)S(1)}, u32[]{:S(2)}, u32[]{:S(2)}) %collective-permute-start.3) | collective-permute-done | bytes 131104 | tf_op jit(solution)/shard_map/ppermute | solution.py:154
  33.0 2.4 %collective-permute-start.4 = (bf16[16,4096]{1,0:T(8,128)(2,1)S(1)}, bf16[16,4096]{1,0:T(8,128)(2,1)S(1)}, u32[]{:S(2)}, u32[]{:S(2)}) collective-permute-start(bf16[16,4096]{1,0:T(8,128)(2,1)S(1)} %fusion.2), channel_id=1, source_target_pairs={{0,16},{8,24},{16,0},{24,8},{1,17},{9,25},{17,1},{25,9},{2,18},{10... | collective-permute-start | bytes 393224 | tf_op jit(solution)/shard_map/ppermute | solution.py:154
  35.5 4.4 %collective-permute-done.4 = bf16[16,4096]{1,0:T(8,128)(2,1)S(1)} collective-permute-done((bf16[16,4096]{1,0:T(8,128)(2,1)S(1)}, bf16[16,4096]{1,0:T(8,128)(2,1)S(1)}, u32[]{:S(2)}, u32[]{:S(2)}) %collective-permute-start.4) | collective-permute-done | bytes 131104 | tf_op jit(solution)/shard_map/ppermute | solution.py:154
  40.2 1.6 %collective-permute-start.5 = (bf16[16,4096]{1,0:T(8,128)(2,1)S(1)}, bf16[16,4096]{1,0:T(8,128)(2,1)S(1)}, u32[]{:S(2)}, u32[]{:S(2)}) collective-permute-start(bf16[16,4096]{1,0:T(8,128)(2,1)S(1)} %multiply_convert_fusion.refs_2_), channel_id=1, source_target_pairs={{0,2},{1,3},{2,0},{3,1},{4,6},{5,7},{6,4},{7,5},{8,10},{9,11},{10,... | collective-permute-start | bytes 393224 | tf_op jit(solution)/shard_map/ppermute | solution.py:154
  41.8 1.5 %collective-permute-start.6 = (bf16[16,4096]{1,0:T(8,128)(2,1)S(1)}, bf16[16,4096]{1,0:T(8,128)(2,1)S(1)}, u32[]{:S(2)}, u32[]{:S(2)}) collective-permute-start(bf16[16,4096]{1,0:T(8,128)(2,1)S(1)} %multiply_convert_fusion.refs_2_), channel_id=1, source_target_pairs={{0,4},{1,5},{2,6},{3,7},{4,0},{5,1},{6,2},{7,3},{8,12},{9,13},{10,... | collective-permute-start | bytes 393224 | tf_op jit(solution)/shard_map/ppermute | solution.py:154
  43.9 1.3 %collective-permute-done.5 = bf16[16,4096]{1,0:T(8,128)(2,1)S(1)} collective-permute-done((bf16[16,4096]{1,0:T(8,128)(2,1)S(1)}, bf16[16,4096]{1,0:T(8,128)(2,1)S(1)}, u32[]{:S(2)}, u32[]{:S(2)}) %collective-permute-start.5) | collective-permute-done | bytes 131104 | tf_op jit(solution)/shard_map/ppermute | solution.py:154
  45.2 1.6 %collective-permute-done.6 = bf16[16,4096]{1,0:T(8,128)(2,1)S(1)} collective-permute-done((bf16[16,4096]{1,0:T(8,128)(2,1)S(1)}, bf16[16,4096]{1,0:T(8,128)(2,1)S(1)}, u32[]{:S(2)}, u32[]{:S(2)}) %collective-permute-start.6) | collective-permute-done | bytes 131104 | tf_op jit(solution)/shard_map/ppermute | solution.py:154
  46.8 2.4 %collective-permute-done.7 = bf16[16,4096]{1,0:T(8,128)(2,1)S(1)} collective-permute-done((bf16[16,4096]{1,0:T(8,128)(2,1)S(1)}, bf16[16,4096]{1,0:T(8,128)(2,1)S(1)}, u32[]{:S(2)}, u32[]{:S(2)}) %collective-permute-start.7) | collective-permute-done | bytes 131104 | tf_op jit(solution)/shard_map/ppermute | solution.py:154
  49.4 3.5 %shard_map.110 = (bf16[4096,512]{1,0:T(8,128)(2,1)S(1)}, bf16[4096,512]{1,0:T(8,128)(2,1)S(1)}) custom-call(bf16[4096,512]{1,0:T(8,128)(2,1)} %bitcast.53, bf16[4096,512]{1,0:T(8,128)(2,1)} %bitcast.54, bf16[16,4096]{1,0:T(8,128)(2,1)S(1)} %multiply_convert_fusion.refs_2_), custom_call_target="tpu_custom_call" | custom-call | bytes 16777216 | tf_op jit(solution)/shard_map/pallas_call | solution.py:37
  52.9 1.7 %shard_map.111 = bf16[64,512]{1,0:T(8,128)(2,1)S(1)} custom-call(bf16[64,4096]{1,0:T(8,128)(2,1)S(1)} %pad_maximum_fusion.rows_ref, bf16[4096,512]{1,0:T(8,128)(2,1)S(1)} %get-tuple-element.11.gate_ref, bf16[4096,512]{1,0:T(8,128)(2,1)S(1)} %get-tuple-element.12.up_ref), custom_call_target="tpu_custom_call" | custom-call | flops 536870912 | bytes 8912896 | tf_op jit(solution)/shard_map/pallas_call | solution.py:60
  54.6 1.7 %shard_map.112 = bf16[64,512]{1,0:T(8,128)(2,1)S(1)} custom-call(bf16[64,4096]{1,0:T(8,128)(2,1)S(1)} %collective-permute-done.8.rows_ref, bf16[4096,512]{1,0:T(8,128)(2,1)S(1)} %get-tuple-element.11.gate_ref, bf16[4096,512]{1,0:T(8,128)(2,1)S(1)} %get-tuple-element.12.up_ref), custom_call_target="tpu_custom_call" | custom-call | flops 536870912 | bytes 8912896 | tf_op jit(solution)/shard_map/pallas_call | solution.py:60
  56.5 1.7 %collective-permute-start.10 = (bf16[80,512]{1,0:T(8,128)(2,1)S(1)}, bf16[80,512]{1,0:T(8,128)(2,1)S(1)}, u32[]{:S(2)}, u32[]{:S(2)}) collective-permute-start(bf16[80,512]{1,0:T(8,128)(2,1)S(1)} %convolution_convert_fusion.refs_1_), channel_id=1, source_target_pairs={{0,16},{8,24},{16,0},{24,8},{1,17},{9,25},{17,1},{25,9},{2,18},{10... | collective-permute-start | bytes 245768 | tf_op jit(solution)/shard_map/ppermute | solution.py:154
  58.2 2.7 %collective-permute-start.9 = (bf16[80,512]{1,0:T(8,128)(2,1)S(1)}, bf16[80,512]{1,0:T(8,128)(2,1)S(1)}, u32[]{:S(2)}, u32[]{:S(2)}) collective-permute-start(bf16[80,512]{1,0:T(8,128)(2,1)S(1)} %convolution_convert_fusion.refs_1_), channel_id=1, source_target_pairs={{0,24},{8,16},{16,8},{24,0},{1,25},{9,17},{17,9},{25,1},{2,26},{10... | collective-permute-start | bytes 245768 | tf_op jit(solution)/shard_map/ppermute | solution.py:154
  61.1 2.2 %shard_map.113.weight_ref = bf16[2,1024,1024]{2,1,0:T(8,128)(2,1)S(1)} custom-call(bf16[2,1024,1024]{2,1,0:T(8,128)(2,1)} %refs_0_.3, bf16[80,512]{1,0:T(8,128)(2,1)S(1)} %convolution_convert_fusion.refs_1_), custom_call_target="tpu_custom_call" | custom-call | bytes 8388608 | tf_op jit(solution)/shard_map/pallas_call | solution.py:37
  63.3 3.0 %collective-permute-done.11 = bf16[80,512]{1,0:T(8,128)(2,1)S(1)} collective-permute-done((bf16[80,512]{1,0:T(8,128)(2,1)S(1)}, bf16[80,512]{1,0:T(8,128)(2,1)S(1)}, u32[]{:S(2)}, u32[]{:S(2)}) %collective-permute-start.11) | collective-permute-done | bytes 81952 | tf_op jit(solution)/shard_map/ppermute | solution.py:154
  66.4 1.3 %shard_map.114 = bf16[2,80,1024]{2,1,0:T(8,128)(2,1)S(1)} custom-call(bf16[2,80,1024]{2,1,0:T(8,128)(2,1)S(1)} %pad_maximum_fusion.1.rows_ref, bf16[2,1024,1024]{2,1,0:T(8,128)(2,1)S(1)} %shard_map.113.weight_ref), custom_call_target="tpu_custom_call" | custom-call | flops 335544320 | bytes 4521984 | tf_op jit(solution)/shard_map/pallas_call | solution.py:60
  68.2 1.3 %collective-permute-done.12 = bf16[64,1024]{1,0:T(8,128)(2,1)S(1)} collective-permute-done((bf16[64,1024]{1,0:T(8,128)(2,1)S(1)}, bf16[64,1024]{1,0:T(8,128)(2,1)S(1)}, u32[]{:S(2)}, u32[]{:S(2)}) %collective-permute-start.12) | collective-permute-done | bytes 131104 | tf_op jit(solution)/shard_map/ppermute | solution.py:154
  70.8 2.4 %collective-permute-start.15 = (bf16[16,1024]{1,0:T(8,128)(2,1)S(1)}, bf16[16,1024]{1,0:T(8,128)(2,1)S(1)}, u32[]{:S(2)}, u32[]{:S(2)}) collective-permute-start(bf16[16,1024]{1,0:T(8,128)(2,1)S(1)} %get-tuple-element.22), channel_id=1, source_target_pairs={{0,6},{1,7},{2,4},{3,5},{4,2},{5,3},{6,0},{7,1},{8,14},{9,15},{10,... | collective-permute-start | bytes 98312 | tf_op jit(solution)/shard_map/ppermute | solution.py:154
  73.6 0.9 %collective-permute-done.14 = bf16[16,1024]{1,0:T(8,128)(2,1)S(1)} collective-permute-done((bf16[16,1024]{1,0:T(8,128)(2,1)S(1)}, bf16[16,1024]{1,0:T(8,128)(2,1)S(1)}, u32[]{:S(2)}, u32[]{:S(2)}) %collective-permute-start.14) | collective-permute-done | bytes 32800 | tf_op jit(solution)/shard_map/ppermute | solution.py:154
  74.5 1.1 %collective-permute-done.15 = bf16[16,1024]{1,0:T(8,128)(2,1)S(1)} collective-permute-done((bf16[16,1024]{1,0:T(8,128)(2,1)S(1)}, bf16[16,1024]{1,0:T(8,128)(2,1)S(1)}, u32[]{:S(2)}, u32[]{:S(2)}) %collective-permute-start.15) | collective-permute-done | bytes 32800 | tf_op jit(solution)/shard_map/ppermute | solution.py:154
  (55 shorter events, 6.4 us)
Async XLA Ops:
  0.0 0.7 copy-start
  4.0 17.3 %all-to-all-start = ((bf16[32,4,384]{2,1,0:T(4,128)(2,1)}), bf16[32,4,384]{2,1,0:T(4,128)(2,1)S(1)}, u32[]{:S(2)}, u32[]{:S(2)}) async-start(bf16[32,4,384]{2,1,0:T(4,128)(2,1)} %bitcast.13), calls=%async_computation | async-start | bytes 196608 | tf_op jit(solution)/shard_map/all_to_all | solution.py:220
  12.2 5.8 %collective-permute-start = (bf16[4,2048]{1,0:T(4,128)(2,1)S(1)}, bf16[4,2048]{1,0:T(4,128)(2,1)S(1)}, u32[]{:S(2)}, u32[]{:S(2)}) collective-permute-start(bf16[4,2048]{1,0:T(4,128)(2,1)S(1)} %get-tuple-element.33), channel_id=1, source_target_pairs={{0,24},{8,16},{16,8},{24,0},{1,25},{9,17},{17,9},{25,1},{2,26},{10... | collective-permute-start | bytes 49160 | tf_op jit(solution)/shard_map/ppermute | solution.py:154
  15.8 4.6 %collective-permute-start.1 = (bf16[4,2048]{1,0:T(4,128)(2,1)S(1)}, bf16[4,2048]{1,0:T(4,128)(2,1)S(1)}, u32[]{:S(2)}, u32[]{:S(2)}) collective-permute-start(bf16[4,2048]{1,0:T(4,128)(2,1)S(1)} %get-tuple-element.32), channel_id=1, source_target_pairs={{0,16},{8,24},{16,0},{24,8},{1,17},{9,25},{17,1},{25,9},{2,18},{10... | collective-permute-start | bytes 49160 | tf_op jit(solution)/shard_map/ppermute | solution.py:154
  15.8 4.6 %collective-permute-start.2 = (bf16[4,2048]{1,0:T(4,128)(2,1)S(1)}, bf16[4,2048]{1,0:T(4,128)(2,1)S(1)}, u32[]{:S(2)}, u32[]{:S(2)}) collective-permute-start(bf16[4,2048]{1,0:T(4,128)(2,1)S(1)} %get-tuple-element.31), channel_id=1, source_target_pairs={{0,8},{8,0},{16,24},{24,16},{1,9},{9,1},{17,25},{25,17},{2,10},{10... | collective-permute-start | bytes 49160 | tf_op jit(solution)/shard_map/ppermute | solution.py:154
  21.4 18.5 %copy-start.1 = (bf16[1,16,4096]{2,1,0:T(8,128)(2,1)S(1)}, bf16[1,16,4096]{2,1,0:T(8,128)(2,1)}, u32[]{:S(2)}) copy-start(bf16[1,16,4096]{2,1,0:T(8,128)(2,1)} %param.14) | copy-start | bytes 393220
  28.0 5.0 %collective-permute-start.3 = (bf16[16,4096]{1,0:T(8,128)(2,1)S(1)}, bf16[16,4096]{1,0:T(8,128)(2,1)S(1)}, u32[]{:S(2)}, u32[]{:S(2)}) collective-permute-start(bf16[16,4096]{1,0:T(8,128)(2,1)S(1)} %get-tuple-element.10), channel_id=1, source_target_pairs={{0,8},{8,0},{16,24},{24,16},{1,9},{9,1},{17,25},{25,17},{2,10},{10... | collective-permute-start | bytes 393224 | tf_op jit(solution)/shard_map/ppermute | solution.py:154
  33.0 6.8 %collective-permute-start.4 = (bf16[16,4096]{1,0:T(8,128)(2,1)S(1)}, bf16[16,4096]{1,0:T(8,128)(2,1)S(1)}, u32[]{:S(2)}, u32[]{:S(2)}) collective-permute-start(bf16[16,4096]{1,0:T(8,128)(2,1)S(1)} %fusion.2), channel_id=1, source_target_pairs={{0,16},{8,24},{16,0},{24,8},{1,17},{9,25},{17,1},{25,9},{2,18},{10... | collective-permute-start | bytes 393224 | tf_op jit(solution)/shard_map/ppermute | solution.py:154
  40.2 5.0 %collective-permute-start.5 = (bf16[16,4096]{1,0:T(8,128)(2,1)S(1)}, bf16[16,4096]{1,0:T(8,128)(2,1)S(1)}, u32[]{:S(2)}, u32[]{:S(2)}) collective-permute-start(bf16[16,4096]{1,0:T(8,128)(2,1)S(1)} %multiply_convert_fusion.refs_2_), channel_id=1, source_target_pairs={{0,2},{1,3},{2,0},{3,1},{4,6},{5,7},{6,4},{7,5},{8,10},{9,11},{10,... | collective-permute-start | bytes 393224 | tf_op jit(solution)/shard_map/ppermute | solution.py:154
  41.8 5.0 %collective-permute-start.6 = (bf16[16,4096]{1,0:T(8,128)(2,1)S(1)}, bf16[16,4096]{1,0:T(8,128)(2,1)S(1)}, u32[]{:S(2)}, u32[]{:S(2)}) collective-permute-start(bf16[16,4096]{1,0:T(8,128)(2,1)S(1)} %multiply_convert_fusion.refs_2_), channel_id=1, source_target_pairs={{0,4},{1,5},{2,6},{3,7},{4,0},{5,1},{6,2},{7,3},{8,12},{9,13},{10,... | collective-permute-start | bytes 393224 | tf_op jit(solution)/shard_map/ppermute | solution.py:154
  43.3 5.9 %collective-permute-start.7 = (bf16[16,4096]{1,0:T(8,128)(2,1)S(1)}, bf16[16,4096]{1,0:T(8,128)(2,1)S(1)}, u32[]{:S(2)}, u32[]{:S(2)}) collective-permute-start(bf16[16,4096]{1,0:T(8,128)(2,1)S(1)} %multiply_convert_fusion.refs_2_), channel_id=1, source_target_pairs={{0,6},{1,7},{2,4},{3,5},{4,2},{5,3},{6,0},{7,1},{8,14},{9,15},{10,... | collective-permute-start | bytes 393224 | tf_op jit(solution)/shard_map/ppermute | solution.py:154
  49.2 5.4 %collective-permute-start.8 = (bf16[64,4096]{1,0:T(8,128)(2,1)S(1)}, bf16[64,4096]{1,0:T(8,128)(2,1)S(1)}, u32[]{:S(2)}, u32[]{:S(2)}) collective-permute-start(bf16[64,4096]{1,0:T(8,128)(2,1)S(1)} %pad_maximum_fusion.rows_ref), channel_id=1, source_target_pairs={{0,1},{1,0},{2,3},{3,2},{4,5},{5,4},{6,7},{7,6},{8,9},{9,8},{10,11... | collective-permute-start | bytes 1572872 | tf_op jit(solution)/shard_map/ppermute | solution.py:154
  56.5 6.8 %collective-permute-start.10 = (bf16[80,512]{1,0:T(8,128)(2,1)S(1)}, bf16[80,512]{1,0:T(8,128)(2,1)S(1)}, u32[]{:S(2)}, u32[]{:S(2)}) collective-permute-start(bf16[80,512]{1,0:T(8,128)(2,1)S(1)} %convolution_convert_fusion.refs_1_), channel_id=1, source_target_pairs={{0,16},{8,24},{16,0},{24,8},{1,17},{9,25},{17,1},{25,9},{2,18},{10... | collective-permute-start | bytes 245768 | tf_op jit(solution)/shard_map/ppermute | solution.py:154
  58.2 8.0 %collective-permute-start.11 = (bf16[80,512]{1,0:T(8,128)(2,1)S(1)}, bf16[80,512]{1,0:T(8,128)(2,1)S(1)}, u32[]{:S(2)}, u32[]{:S(2)}) collective-permute-start(bf16[80,512]{1,0:T(8,128)(2,1)S(1)} %convolution_convert_fusion.refs_1_), channel_id=1, source_target_pairs={{0,8},{8,0},{16,24},{24,16},{1,9},{9,1},{17,25},{25,17},{2,10},{10... | collective-permute-start | bytes 245768 | tf_op jit(solution)/shard_map/ppermute | solution.py:154
  58.2 8.0 %collective-permute-start.9 = (bf16[80,512]{1,0:T(8,128)(2,1)S(1)}, bf16[80,512]{1,0:T(8,128)(2,1)S(1)}, u32[]{:S(2)}, u32[]{:S(2)}) collective-permute-start(bf16[80,512]{1,0:T(8,128)(2,1)S(1)} %convolution_convert_fusion.refs_1_), channel_id=1, source_target_pairs={{0,24},{8,16},{16,8},{24,0},{1,25},{9,17},{17,9},{25,1},{2,26},{10... | collective-permute-start | bytes 245768 | tf_op jit(solution)/shard_map/ppermute | solution.py:154
  68.2 1.4 %collective-permute-start.12 = (bf16[64,1024]{1,0:T(8,128)(2,1)S(1)}, bf16[64,1024]{1,0:T(8,128)(2,1)S(1)}, u32[]{:S(2)}, u32[]{:S(2)}) collective-permute-start(bf16[64,1024]{1,0:T(8,128)(2,1)S(1)} %slice.134), channel_id=1, source_target_pairs={{0,1},{1,0},{2,3},{3,2},{4,5},{5,4},{6,7},{7,6},{8,9},{9,8},{10,11... | collective-permute-start | bytes 393224 | tf_op jit(solution)/shard_map/ppermute | solution.py:154
  69.6 4.0 %collective-permute-start.13 = (bf16[16,1024]{1,0:T(8,128)(2,1)S(1)}, bf16[16,1024]{1,0:T(8,128)(2,1)S(1)}, u32[]{:S(2)}, u32[]{:S(2)}) collective-permute-start(bf16[16,1024]{1,0:T(8,128)(2,1)S(1)} %get-tuple-element.21), channel_id=1, source_target_pairs={{0,2},{1,3},{2,0},{3,1},{4,6},{5,7},{6,4},{7,5},{8,10},{9,11},{10,... | collective-permute-start | bytes 98312 | tf_op jit(solution)/shard_map/ppermute | solution.py:154
  70.2 4.3 %collective-permute-start.14 = (bf16[16,1024]{1,0:T(8,128)(2,1)S(1)}, bf16[16,1024]{1,0:T(8,128)(2,1)S(1)}, u32[]{:S(2)}, u32[]{:S(2)}) collective-permute-start(bf16[16,1024]{1,0:T(8,128)(2,1)S(1)} %get-tuple-element.23), channel_id=1, source_target_pairs={{0,4},{1,5},{2,6},{3,7},{4,0},{5,1},{6,2},{7,3},{8,12},{9,13},{10,... | collective-permute-start | bytes 98312 | tf_op jit(solution)/shard_map/ppermute | solution.py:154
  70.8 4.8 %collective-permute-start.15 = (bf16[16,1024]{1,0:T(8,128)(2,1)S(1)}, bf16[16,1024]{1,0:T(8,128)(2,1)S(1)}, u32[]{:S(2)}, u32[]{:S(2)}) collective-permute-start(bf16[16,1024]{1,0:T(8,128)(2,1)S(1)} %get-tuple-element.22), channel_id=1, source_target_pairs={{0,6},{1,7},{2,4},{3,5},{4,2},{5,3},{6,0},{7,1},{8,14},{9,15},{10,... | collective-permute-start | bytes 98312 | tf_op jit(solution)/shard_map/ppermute | solution.py:154

commit v3 on v2

--- a/solution.py
+++ b/solution.py
@@ -1,3 +1,5 @@
+import functools
+
 import jax
 import jax.numpy as jnp
 from jax import lax
@@ -71,6 +73,57 @@
 
 def column_tile(width):
     return next(tile for tile in (512, 256, 128, width) if width % tile == 0)
+
+
+def prepare_body(experts, q_hbm, k_hbm, v_hbm, ids_hbm, weights_hbm, *refs):
+    *q_outs, parts_ref, k_ref, v_ref, ids_ref, weights_ref, sems = refs
+    seq_count, s = lax.axis_size("seq"), lax.axis_index("seq")
+    exp_count = lax.axis_size("exp")
+    tok_dev, width = q_outs[0].shape
+    copies = [
+        pltpu.make_async_copy(source, target, sems.at[i])
+        for i, (source, target) in enumerate(
+            [(ids_hbm, ids_ref), (weights_hbm, weights_ref), (k_hbm, k_ref), (v_hbm, v_ref)]
+        )
+    ]
+    for k, q_out in enumerate(q_outs):
+        cut = pl.ds(pl.multiple_of((s ^ k) * width, 128), width)
+        copies.append(pltpu.make_async_copy(q_hbm.at[:, cut], q_out, sems.at[4 + k]))
+    for copy in copies:
+        copy.start()
+    copies[0].wait()
+    copies[1].wait()
+
+    lanes = parts_ref.shape[2] - 2 * HEAD_DIM
+    count = ids_ref.shape[1]
+    line = lax.broadcasted_iota(jnp.int32, (lanes, count), 0)
+    table = jnp.zeros(line.shape, jnp.float32)
+    for j in range(ids_ref.shape[0]):
+        named = ids_ref[j : j + 1, :] == line % experts
+        table = table + jnp.where(named, weights_ref[j : j + 1, :], 0.0)
+    high = table.astype(jnp.bfloat16).astype(jnp.float32)
+    middle = (table - high).astype(jnp.bfloat16).astype(jnp.float32)
+    low = table - high - middle
+    term = line // experts
+    packed = jnp.where(
+        term == 0, high, jnp.where(term == 1, middle, jnp.where(term == 2, low, 0.0))
+    ).astype(jnp.bfloat16)
+    turn = lax.broadcasted_iota(jnp.int32, (count, count), 0) + s * tok_dev
+    turn = (turn == lax.broadcasted_iota(jnp.int32, (count, count), 1)).astype(jnp.bfloat16)
+    own = lax.dot_general(
+        turn, packed, (((1,), (1,)), ((), ())), preferred_element_type=jnp.float32
+    )
+    own = own[:tok_dev].astype(jnp.bfloat16)
+    copies[2].wait()
+    copies[3].wait()
+    reps = seq_count // KV_HEADS
+    for j in range(seq_count):
+        cut = slice(j // reps * HEAD_DIM, (j // reps + 1) * HEAD_DIM)
+        part = jnp.concatenate([k_ref[:, cut], v_ref[:, cut], own], axis=1)
+        for i in range(exp_count):
+            parts_ref[j * exp_count + i] = part
+    for copy in copies[4:]:
+        copy.wait()
 
 
 def attend_body(rows_ref, pairs_ref, *refs):
@@ -135,15 +188,27 @@
     lax.fori_loop(0, width // tile, step, 0)
 
 
-def down_body(rows_ref, weight_ref, out_ref):
+def down_body(rows_ref, weight_ref, combine_ref, near_ref, far_ref):
     count, _, width = weight_ref.shape
     tile = min(256, column_tile(width))
+    half = near_ref.shape[0]
+    high = combine_ref[...].astype(jnp.bfloat16)
+    rest = combine_ref[...] - high.astype(jnp.float32)
+    middle = rest.astype(jnp.bfloat16)
+    low = (rest - middle.astype(jnp.float32)).astype(jnp.bfloat16)
 
     def step(i, carry):
         cols = pl.ds(pl.multiple_of(i * tile, tile), tile)
-        for p in range(count):
-            out = jnp.dot(rows_ref[p], weight_ref[p, :, cols], preferred_element_type=jnp.float32)
-            out_ref[p, :, cols] = out.astype(out_ref.dtype)
+        outs = [
+            jnp.dot(rows_ref[p], weight_ref[p, :, cols], preferred_element_type=jnp.float32)
+            for p in range(count)
+        ]
+        outs = jnp.concatenate(outs, axis=0).astype(jnp.bfloat16)
+        total = sum(
+            jnp.dot(term, outs, preferred_element_type=jnp.float32) for term in (low, middle, high)
+        )
+        near_ref[:, cols] = total[:half]
+        far_ref[:, cols] = total[half:].astype(far_ref.dtype)
         return carry
 
     lax.fori_loop(0, width // tile, step, 0)
@@ -190,36 +255,30 @@
     tokens = exp_count * column
 
     width = head_dev * HEAD_DIM
-    q_rows = queries[0]
-    pieces = []
-    for k in range(seq_count):
-        piece = lax.dynamic_slice_in_dim(q_rows, (s ^ k) * width, width, 1)
-        pieces.append(piece if k == 0 else exchange(piece, "seq", k))
-
-    expert_of = lax.iota(jnp.int32, experts)
-    own_ids = lax.dynamic_slice_in_dim(expert_ids[0], s * tok_dev, tok_dev, 0)
-    own_weights = lax.dynamic_slice_in_dim(route_weights[0], s * tok_dev, tok_dev, 0)
-    table = jnp.sum(
-        jnp.where(own_ids[:, :, None] == expert_of[None, None, :], own_weights[:, :, None], 0.0),
-        axis=1,
-    )
-    high = lax.reduce_precision(table, 8, 7)
-    middle = lax.reduce_precision(table - high, 8, 7)
-    low = table - high - middle
-    packed = jnp.concatenate([high, middle, low], axis=1).astype(bf16)
-    packed = jnp.pad(packed, ((0, 0), (0, -packed.shape[1] % 128)))
-
-    reps = seq_count // KV_HEADS
-    parts = []
-    for j in range(seq_count):
-        cut = slice(j // reps * HEAD_DIM, (j // reps + 1) * HEAD_DIM)
-        parts.append(jnp.concatenate([key_rows[0][:, cut], values[0][:, cut], packed], axis=1))
-    parts = jnp.stack(parts, axis=0)
-    parts = jnp.broadcast_to(parts[:, None], (seq_count, exp_count) + parts.shape[1:])
-    parts = parts.reshape((seq_count * exp_count,) + parts.shape[2:])
+    lanes = 3 * experts + -3 * experts % 128
+    pair = 2 * HEAD_DIM + lanes
+    sources = [
+        queries[0],
+        key_rows[0],
+        values[0],
+        expert_ids[0].T,
+        route_weights[0].T,
+    ]
+    *pieces, parts = pl.pallas_call(
+        functools.partial(prepare_body, experts),
+        out_shape=[pltpu.VMEM((tok_dev, width), bf16)] * seq_count
+        + [pltpu.VMEM((seq_count * exp_count, tok_dev, pair), bf16)],
+        in_specs=[pl.BlockSpec(memory_space=pltpu.HBM)] * len(sources),
+        out_specs=[pl.BlockSpec(memory_space=pltpu.VMEM)] * (seq_count + 1),
+        scratch_shapes=[pltpu.VMEM(a.shape, a.dtype) for a in sources[1:]]
+        + [pltpu.SemaphoreType.DMA((4 + seq_count,))],
+        compiler_params=pltpu.CompilerParams(vmem_limit_bytes=2 << 20),
+    )(*[in_hbm(a) for a in sources])
     gathered = lax.all_to_all(parts, ("seq", "exp"), split_axis=0, concat_axis=0, tiled=True)
     gathered = gathered.reshape(tokens, gathered.shape[2])
+    pieces = pieces[:1] + [exchange(pieces[k], "seq", k) for k in range(1, seq_count)]
     rows = jnp.concatenate(in_order(pieces, s), axis=0)
+
     row = lax.iota(jnp.int32, tokens)
     key_pos = gathered_pos(row, tok_dev, exp_count, column)
     position = row
@@ -246,14 +305,18 @@
         streamed=[out_proj],
         limit=24 << 20,
     )
+    gate_local, gain = fetch([gate_weight[0, 0], norm_gain], sent)
     step = 1
     while step < seq_count:
-        projected = projected + exchange(sent, "seq", step).astype(f32)
+        arrived = exchange(sent, "seq", step)
+        projected = projected + arrived.astype(f32)
         sent = projected.astype(bf16)
+        if step == 1:
+            (up_local,) = fetch([up_weight[0, 0]], sent)
         step *= 2
     hidden_one = residual[0].astype(f32) + projected
     mean_square = jnp.mean(hidden_one * hidden_one, axis=1, keepdims=True)
-    normed = (hidden_one * lax.rsqrt(mean_square + norm_eps) * norm_gain.astype(f32)).astype(bf16)
+    normed = (hidden_one * lax.rsqrt(mean_square + norm_eps) * gain.astype(f32)).astype(bf16)
     col_width = down_weight.shape[2]
     kept = lax.dynamic_slice_in_dim(hidden_one, s * col_width, col_width, 1)
 
@@ -280,7 +343,6 @@
     )
 
     near = [normed] + [exchange(normed, "exp", k) for k in range(2, exp_count, 2)]
-    gate_local, up_local = fetch([gate_weight[0, 0], up_weight[0, 0]], normed)
     near = jnp.concatenate(near, axis=0)
     far = exchange(near, "exp", 1)
 
@@ -303,19 +365,16 @@
     rows_in = jnp.stack(
         [jnp.concatenate(pieces[p * group : (p + 1) * group], axis=1) for p in range(exp_dev)], axis=0
     )
-    (outputs,) = local_call(
+    mid = half * column
+    routed, far = local_call(
         down_body,
-        [((exp_dev, slots, col_width), bf16)],
+        [((mid, col_width), f32), ((mid, col_width), bf16)],
         rows_in,
         down_local,
+        combine,
         flops=2 * slots * down_weight.size,
     )
-    outputs = outputs.reshape(exp_dev * slots, col_width)
-    routed = jnp.dot(
-        combine, outputs.astype(f32), precision=lax.Precision.HIGHEST, preferred_element_type=f32
-    )
-    mid = half * column
-    routed = routed[:mid] + exchange(routed[mid:].astype(bf16), "exp", 1).astype(f32)
+    routed = routed + exchange(far, "exp", 1).astype(f32)
     result = kept + routed[:column]
     for i in range(1, half):
         part = routed[i * column : (i + 1) * column].astype(bf16)

time: 76.8 us -> 77.1 us (level)
  waiting for transfers between devices: 24.1 us -> 29.4 us
  local copies, waits for them, and re-layouts: 3.93 us -> 0.06 us
  Pallas kernels: 17.1 us -> 20.5 us
  other arithmetic: 3.78 us -> 1.54 us
  starting transfers between devices: 26 us -> 24.4 us
    all_to_all x1, waiting for transfers between devices: 0.01 us -> 7.58 us  [compact(): lax.all_to_all(parts, ('seq', 'exp'), split_axis=0, concat_axis=0, tiled=...]
    ppermute x16, waiting for transfers between devices: 24.1 us -> 21.8 us  [exchange(): return lax.ppermute(value, axis, [(i, i ^ step) for i in range(count)])]
    dynamic_slice x5 -> x0, local copies, waits for them, and re-layouts: 1.78 us -> none  [the longest x2 0.84 us: compact(): lax.dynamic_slice_in_dim(route_weights[0], s * tok_dev, tok_dev, 0)]
    pallas_call x0 -> x1, Pallas kernels: none -> 1.6 us  [compact(): pl.pallas_call(functools.partial(prepare_body, experts), out_shape=[pltpu...]
    all_to_all x1, starting transfers between devices: 7.33 us -> 5.99 us  [compact(): lax.all_to_all(parts, ('seq', 'exp'), split_axis=0, concat_axis=0, tiled=...]
    pallas_call x4, Pallas kernels: 11.4 us -> 12.3 us  [local_call(): pl.pallas_call(body, out_shape=[pltpu.VMEM(shape, dtype) for shape, dtype...]
    pallas_call x2 -> x3, Pallas kernels: 5.69 us -> 6.61 us  [fetch(): pl.pallas_call(body, out_shape=[pltpu.VMEM(shape, sources[0].dtype) for s...]
    slice x1 -> x0, other arithmetic: 0.8 us -> none  [compact(): key_rows[0][:, cut]]
  transfers between devices with their start and end apart: 17 -> 17, of which waited for: 12 -> 11; matrix products, arithmetic and copies ran while one was open for 4% -> 1% of each run, Pallas kernels for 10% -> 11%
where the time goes in v3:
time: 77.1 us; the launch traced here: 76.8 us
  waiting for transfers between devices  29.4 us (38%)
  starting transfers between devices  24.4 us (32%)
  Pallas kernels  20.5 us (27%)
  other arithmetic  1.54 us (2%)
    ppermute x16, waiting for transfers between devices, exchange(): return lax.ppermute(value, axis, [(i, i ^ step) for i in range(count)])  21.8 us
    ppermute x16, starting transfers between devices, exchange(): return lax.ppermute(value, axis, [(i, i ^ step) for i in range(count)])  18.4 us
    pallas_call x4, Pallas kernels, local_call(): pl.pallas_call(body, out_shape=[pltpu.VMEM(shape, dtype) for shape, dtype...  12.3 us
    all_to_all x1, waiting for transfers between devices, compact(): lax.all_to_all(parts, ('seq', 'exp'), split_axis=0, concat_axis=0, tiled=...  7.58 us
    pallas_call x3, Pallas kernels, fetch(): pl.pallas_call(body, out_shape=[pltpu.VMEM(shape, sources[0].dtype) for s...  6.61 us
    all_to_all x1, starting transfers between devices, compact(): lax.all_to_all(parts, ('seq', 'exp'), split_axis=0, concat_axis=0, tiled=...  5.99 us
    pallas_call x1, Pallas kernels, compact(): pl.pallas_call(functools.partial(prepare_body, experts), out_shape=[pltpu...  1.6 us
  transfers between devices with their start and end apart: 17, of which 11 were waited for; matrix products, arithmetic and copies ran while one was open for 1% of the time, Pallas kernels for 11%

profile of v3, /device:TPU:0, one launch (start us, length us, event | category | flops | bytes accessed | tf_op | source)
XLA Modules:
  0.0 76.8 jit_solution(13192139894011868744)
XLA Ops:
  0.0 1.6 %shard_map.109 = (bf16[4,2048]{1,0:T(4,128)(2,1)S(1)}, bf16[4,2048]{1,0:T(4,128)(2,1)S(1)}, bf16[4,2048]{1,0:T(4,128)(2,1)S(1)}, bf16[4,2048]{1,0:T(4,128)(2,1)S(1)}, bf16[32,4,384]{2,1,0:T(4,128)(2,1)}) custom-call(bf16[4,8192]{1,0:T(4,128)(2,1)} %bitcast.31, bf16[4,512]{1,0:T(4,128)(2,1)} %bitcast.32, bf16[4,512]{1,0:T(4,128)(2,1)} %bitcast.33, ...), custom_call_target="tpu_custom_call" | custom-call | tf_op jit(solution)/shard_map/pallas_call | solution.py:267
  1.6 5.1 %collective-permute-start = (bf16[4,2048]{1,0:T(4,128)(2,1)S(1)}, bf16[4,2048]{1,0:T(4,128)(2,1)S(1)}, u32[]{:S(2)}, u32[]{:S(2)}) collective-permute-start(bf16[4,2048]{1,0:T(4,128)(2,1)S(1)} %get-tuple-element.16), channel_id=1, source_target_pairs={{0,24},{8,16},{16,8},{24,0},{1,25},{9,17},{17,9},{25,1},{2,26},{10... | collective-permute-start | bytes 49160 | tf_op jit(solution)/shard_map/ppermute | solution.py:219
  6.8 0.6 collective-permute-start.2
  7.4 6.0 %all-to-all-start = ((bf16[32,4,384]{2,1,0:T(4,128)(2,1)}), bf16[32,4,384]{2,1,0:T(4,128)(2,1)S(1)}, u32[]{:S(2)}, u32[]{:S(2)}) async-start(bf16[32,4,384]{2,1,0:T(4,128)(2,1)} %get-tuple-element.20), calls=%async_computation | async-start | bytes 196608 | tf_op jit(solution)/shard_map/all_to_all | solution.py:277
  13.6 7.6 %all-to-all-done = bf16[32,4,384]{2,1,0:T(4,128)(2,1)S(1)} async-done(((bf16[32,4,384]{2,1,0:T(4,128)(2,1)}), bf16[32,4,384]{2,1,0:T(4,128)(2,1)S(1)}, u32[]{:S(2)}, u32[]{:S(2)}) %all-to-all-start) | async-done | bytes 98336 | tf_op jit(solution)/shard_map/all_to_all | solution.py:277
  21.2 6.6 %shard_map.110 = (f32[16,4096]{1,0:T(8,128)S(1)}, bf16[16,4096]{1,0:T(8,128)(2,1)S(1)}) custom-call(bf16[16,2048]{1,0:T(8,128)(2,1)S(1)} %pad_maximum_fusion.3.rows_ref, bf16[128,256]{1,0:T(8,128)(2,1)S(1)} %slice.55.pairs_ref, bf16[2048,4096]{1,0:T(8,128)(2,1)} %refs_0_.2), custom_call_target="tpu_custom_call" | custom-call | flops 268435456 | bytes 16908288 | tf_op jit(solution)/shard_map/pallas_call | solution.py:62
  27.8 0.7 collective-permute-start.3
  28.8 2.2 %shard_map.111 = (bf16[4096,512]{1,0:T(8,128)(2,1)S(1)}, bf16[4096]{0:T(1024)(128)(2,1)S(1)}) custom-call(bf16[4096,512]{1,0:T(8,128)(2,1)} %bitcast.29, bf16[4096]{0:T(1024)(128)(2,1)} %refs_1_.1, bf16[16,4096]{1,0:T(8,128)(2,1)S(1)} %get-tuple-element.22.refs_2_), custom_call_target="tpu_custom_call" | custom-call | bytes 8404992 | tf_op jit(solution)/shard_map/pallas_call | solution.py:39
  31.0 2.4 %collective-permute-done.3 = bf16[16,4096]{1,0:T(8,128)(2,1)S(1)} collective-permute-done((bf16[16,4096]{1,0:T(8,128)(2,1)S(1)}, bf16[16,4096]{1,0:T(8,128)(2,1)S(1)}, u32[]{:S(2)}, u32[]{:S(2)}) %collective-permute-start.3) | collective-permute-done | bytes 131104 | tf_op jit(solution)/shard_map/ppermute | solution.py:219
  33.9 7.3 %collective-permute-done.4 = bf16[16,4096]{1,0:T(8,128)(2,1)S(1)} collective-permute-done((bf16[16,4096]{1,0:T(8,128)(2,1)S(1)}, bf16[16,4096]{1,0:T(8,128)(2,1)S(1)}, u32[]{:S(2)}, u32[]{:S(2)}) %collective-permute-start.4) | collective-permute-done | bytes 131104 | tf_op jit(solution)/shard_map/ppermute | solution.py:219
  41.6 1.1 %collective-permute-start.5 = (bf16[16,4096]{1,0:T(8,128)(2,1)S(1)}, bf16[16,4096]{1,0:T(8,128)(2,1)S(1)}, u32[]{:S(2)}, u32[]{:S(2)}) collective-permute-start(bf16[16,4096]{1,0:T(8,128)(2,1)S(1)} %multiply_convert_fusion), channel_id=1, source_target_pairs={{0,2},{1,3},{2,0},{3,1},{4,6},{5,7},{6,4},{7,5},{8,10},{9,11},{10,... | collective-permute-start | bytes 393224 | tf_op jit(solution)/shard_map/ppermute | solution.py:219
  42.7 0.6 collective-permute-start.6
  43.2 1.9 %collective-permute-start.7 = (bf16[16,4096]{1,0:T(8,128)(2,1)S(1)}, bf16[16,4096]{1,0:T(8,128)(2,1)S(1)}, u32[]{:S(2)}, u32[]{:S(2)}) collective-permute-start(bf16[16,4096]{1,0:T(8,128)(2,1)S(1)} %multiply_convert_fusion), channel_id=1, source_target_pairs={{0,6},{1,7},{2,4},{3,5},{4,2},{5,3},{6,0},{7,1},{8,14},{9,15},{10,... | collective-permute-start | bytes 393224 | tf_op jit(solution)/shard_map/ppermute | solution.py:219
  45.1 2.0 %collective-permute-done.5 = bf16[16,4096]{1,0:T(8,128)(2,1)S(1)} collective-permute-done((bf16[16,4096]{1,0:T(8,128)(2,1)S(1)}, bf16[16,4096]{1,0:T(8,128)(2,1)S(1)}, u32[]{:S(2)}, u32[]{:S(2)}) %collective-permute-start.5) | collective-permute-done | bytes 131104 | tf_op jit(solution)/shard_map/ppermute | solution.py:219
  47.2 3.3 %collective-permute-done.6 = bf16[16,4096]{1,0:T(8,128)(2,1)S(1)} collective-permute-done((bf16[16,4096]{1,0:T(8,128)(2,1)S(1)}, bf16[16,4096]{1,0:T(8,128)(2,1)S(1)}, u32[]{:S(2)}, u32[]{:S(2)}) %collective-permute-start.6) | collective-permute-done | bytes 131104 | tf_op jit(solution)/shard_map/ppermute | solution.py:219
  50.8 2.2 %shard_map.112.up_ref = bf16[4096,512]{1,0:T(8,128)(2,1)S(1)} custom-call(bf16[4096,512]{1,0:T(8,128)(2,1)} %bitcast.30, bf16[16,4096]{1,0:T(8,128)(2,1)S(1)} %fusion.2.refs_1_), custom_call_target="tpu_custom_call" | custom-call | bytes 8388608 | tf_op jit(solution)/shard_map/pallas_call | solution.py:39
  53.0 1.7 %shard_map.113 = bf16[64,512]{1,0:T(8,128)(2,1)S(1)} custom-call(bf16[64,4096]{1,0:T(8,128)(2,1)S(1)} %pad_maximum_fusion.rows_ref, bf16[4096,512]{1,0:T(8,128)(2,1)S(1)} %get-tuple-element.24.gate_ref, bf16[4096,512]{1,0:T(8,128)(2,1)S(1)} %shard_map.112.up_ref), custom_call_target="tpu_custom_call" | custom-call | flops 536870912 | bytes 8912896 | tf_op jit(solution)/shard_map/pallas_call | solution.py:62
  54.8 1.7 %shard_map.114 = bf16[64,512]{1,0:T(8,128)(2,1)S(1)} custom-call(bf16[64,4096]{1,0:T(8,128)(2,1)S(1)} %collective-permute-done.8.rows_ref, bf16[4096,512]{1,0:T(8,128)(2,1)S(1)} %get-tuple-element.24.gate_ref, bf16[4096,512]{1,0:T(8,128)(2,1)S(1)} %shard_map.112.up_ref), custom_call_target="tpu_custom_call" | custom-call | flops 536870912 | bytes 8912896 | tf_op jit(solution)/shard_map/pallas_call | solution.py:62
  56.7 1.5 %collective-permute-start.11 = (bf16[80,512]{1,0:T(8,128)(2,1)S(1)}, bf16[80,512]{1,0:T(8,128)(2,1)S(1)}, u32[]{:S(2)}, u32[]{:S(2)}) collective-permute-start(bf16[80,512]{1,0:T(8,128)(2,1)S(1)} %convolution_convert_fusion.refs_1_), channel_id=1, source_target_pairs={{0,8},{8,0},{16,24},{24,16},{1,9},{9,1},{17,25},{25,17},{2,10},{10... | collective-permute-start | bytes 245768 | tf_op jit(solution)/shard_map/ppermute | solution.py:219
  58.2 2.9 %collective-permute-start.9 = (bf16[80,512]{1,0:T(8,128)(2,1)S(1)}, bf16[80,512]{1,0:T(8,128)(2,1)S(1)}, u32[]{:S(2)}, u32[]{:S(2)}) collective-permute-start(bf16[80,512]{1,0:T(8,128)(2,1)S(1)} %convolution_convert_fusion.refs_1_), channel_id=1, source_target_pairs={{0,24},{8,16},{16,8},{24,0},{1,25},{9,17},{17,9},{25,1},{2,26},{10... | collective-permute-start | bytes 245768 | tf_op jit(solution)/shard_map/ppermute | solution.py:219
  61.2 2.2 %shard_map.115.weight_ref = bf16[2,1024,1024]{2,1,0:T(8,128)(2,1)S(1)} custom-call(bf16[2,1024,1024]{2,1,0:T(8,128)(2,1)} %refs_0_.3, bf16[80,512]{1,0:T(8,128)(2,1)S(1)} %convolution_convert_fusion.refs_1_), custom_call_target="tpu_custom_call" | custom-call | bytes 8388608 | tf_op jit(solution)/shard_map/pallas_call | solution.py:39
  63.4 0.5 collective-permute-done.11
  63.9 1.6 %collective-permute-done.9 = bf16[80,512]{1,0:T(8,128)(2,1)S(1)} collective-permute-done((bf16[80,512]{1,0:T(8,128)(2,1)S(1)}, bf16[80,512]{1,0:T(8,128)(2,1)S(1)}, u32[]{:S(2)}, u32[]{:S(2)}) %collective-permute-start.9) | collective-permute-done | bytes 81952 | tf_op jit(solution)/shard_map/ppermute | solution.py:219
  65.6 2.3 %shard_map.116 = (f32[64,1024]{1,0:T(8,128)S(1)}, bf16[64,1024]{1,0:T(8,128)(2,1)S(1)}) custom-call(bf16[2,80,1024]{2,1,0:T(8,128)(2,1)S(1)} %pad_maximum_fusion.1.rows_ref, bf16[2,1024,1024]{2,1,0:T(8,128)(2,1)S(1)} %shard_map.115.weight_ref, f32[128,160]{1,0:T(8,128)S(1)} %pad_maximum_fusion.2.combine_ref), custom_call_target="tpu_custom_call" | custom-call | flops 335544320 | bytes 4603904 | tf_op jit(solution)/shard_map/pallas_call | solution.py:62
  68.0 1.3 %collective-permute-done.12 = bf16[64,1024]{1,0:T(8,128)(2,1)S(1)} collective-permute-done((bf16[64,1024]{1,0:T(8,128)(2,1)S(1)}, bf16[64,1024]{1,0:T(8,128)(2,1)S(1)}, u32[]{:S(2)}, u32[]{:S(2)}) %collective-permute-start.12) | collective-permute-done | bytes 131104 | tf_op jit(solution)/shard_map/ppermute | solution.py:219
  69.4 1.0 %collective-permute-start.13 = (bf16[16,1024]{1,0:T(8,128)(2,1)S(1)}, bf16[16,1024]{1,0:T(8,128)(2,1)S(1)}, u32[]{:S(2)}, u32[]{:S(2)}) collective-permute-start(bf16[16,1024]{1,0:T(8,128)(2,1)S(1)} %get-tuple-element.35), channel_id=1, source_target_pairs={{0,2},{1,3},{2,0},{3,1},{4,6},{5,7},{6,4},{7,5},{8,10},{9,11},{10,... | collective-permute-start | bytes 98312 | tf_op jit(solution)/shard_map/ppermute | solution.py:219
  70.4 1.0 %collective-permute-start.14 = (bf16[16,1024]{1,0:T(8,128)(2,1)S(1)}, bf16[16,1024]{1,0:T(8,128)(2,1)S(1)}, u32[]{:S(2)}, u32[]{:S(2)}) collective-permute-start(bf16[16,1024]{1,0:T(8,128)(2,1)S(1)} %get-tuple-element.37), channel_id=1, source_target_pairs={{0,4},{1,5},{2,6},{3,7},{4,0},{5,1},{6,2},{7,3},{8,12},{9,13},{10,... | collective-permute-start | bytes 98312 | tf_op jit(solution)/shard_map/ppermute | solution.py:219
  71.4 1.5 %collective-permute-start.15 = (bf16[16,1024]{1,0:T(8,128)(2,1)S(1)}, bf16[16,1024]{1,0:T(8,128)(2,1)S(1)}, u32[]{:S(2)}, u32[]{:S(2)}) collective-permute-start(bf16[16,1024]{1,0:T(8,128)(2,1)S(1)} %get-tuple-element.36), channel_id=1, source_target_pairs={{0,6},{1,7},{2,4},{3,5},{4,2},{5,3},{6,0},{7,1},{8,14},{9,15},{10,... | collective-permute-start | bytes 98312 | tf_op jit(solution)/shard_map/ppermute | solution.py:219
  72.9 0.4 collective-permute-done.13
  73.3 1.0 %collective-permute-done.14 = bf16[16,1024]{1,0:T(8,128)(2,1)S(1)} collective-permute-done((bf16[16,1024]{1,0:T(8,128)(2,1)S(1)}, bf16[16,1024]{1,0:T(8,128)(2,1)S(1)}, u32[]{:S(2)}, u32[]{:S(2)}) %collective-permute-start.14) | collective-permute-done | bytes 32800 | tf_op jit(solution)/shard_map/ppermute | solution.py:219
  74.3 1.9 %collective-permute-done.15 = bf16[16,1024]{1,0:T(8,128)(2,1)S(1)} collective-permute-done((bf16[16,1024]{1,0:T(8,128)(2,1)S(1)}, bf16[16,1024]{1,0:T(8,128)(2,1)S(1)}, u32[]{:S(2)}, u32[]{:S(2)}) %collective-permute-start.15) | collective-permute-done | bytes 32800 | tf_op jit(solution)/shard_map/ppermute | solution.py:219
  76.2 0.6 fusion.17
  (42 shorter events, 2.0 us)
Async XLA Ops:
  1.6 11.9 %collective-permute-start = (bf16[4,2048]{1,0:T(4,128)(2,1)S(1)}, bf16[4,2048]{1,0:T(4,128)(2,1)S(1)}, u32[]{:S(2)}, u32[]{:S(2)}) collective-permute-start(bf16[4,2048]{1,0:T(4,128)(2,1)S(1)} %get-tuple-element.16), channel_id=1, source_target_pairs={{0,24},{8,16},{16,8},{24,0},{1,25},{9,17},{17,9},{25,1},{2,26},{10... | collective-permute-start | bytes 49160 | tf_op jit(solution)/shard_map/ppermute | solution.py:219
  6.7 6.7 %collective-permute-start.1 = (bf16[4,2048]{1,0:T(4,128)(2,1)S(1)}, bf16[4,2048]{1,0:T(4,128)(2,1)S(1)}, u32[]{:S(2)}, u32[]{:S(2)}) collective-permute-start(bf16[4,2048]{1,0:T(4,128)(2,1)S(1)} %get-tuple-element.17), channel_id=1, source_target_pairs={{0,16},{8,24},{16,0},{24,8},{1,17},{9,25},{17,1},{25,9},{2,18},{10... | collective-permute-start | bytes 49160 | tf_op jit(solution)/shard_map/ppermute | solution.py:219
  6.8 6.7 %collective-permute-start.2 = (bf16[4,2048]{1,0:T(4,128)(2,1)S(1)}, bf16[4,2048]{1,0:T(4,128)(2,1)S(1)}, u32[]{:S(2)}, u32[]{:S(2)}) collective-permute-start(bf16[4,2048]{1,0:T(4,128)(2,1)S(1)} %get-tuple-element.18), channel_id=1, source_target_pairs={{0,8},{8,0},{16,24},{24,16},{1,9},{9,1},{17,25},{25,17},{2,10},{10... | collective-permute-start | bytes 49160 | tf_op jit(solution)/shard_map/ppermute | solution.py:219
  7.4 13.8 %all-to-all-start = ((bf16[32,4,384]{2,1,0:T(4,128)(2,1)}), bf16[32,4,384]{2,1,0:T(4,128)(2,1)S(1)}, u32[]{:S(2)}, u32[]{:S(2)}) async-start(bf16[32,4,384]{2,1,0:T(4,128)(2,1)} %get-tuple-element.20), calls=%async_computation | async-start | bytes 196608 | tf_op jit(solution)/shard_map/all_to_all | solution.py:277
  27.8 13.4 %copy-start = (bf16[1,16,4096]{2,1,0:T(8,128)(2,1)S(1)}, bf16[1,16,4096]{2,1,0:T(8,128)(2,1)}, u32[]{:S(2)}) copy-start(bf16[1,16,4096]{2,1,0:T(8,128)(2,1)} %param.14) | copy-start | bytes 393220
  27.8 5.6 %collective-permute-start.3 = (bf16[16,4096]{1,0:T(8,128)(2,1)S(1)}, bf16[16,4096]{1,0:T(8,128)(2,1)S(1)}, u32[]{:S(2)}, u32[]{:S(2)}) collective-permute-start(bf16[16,4096]{1,0:T(8,128)(2,1)S(1)} %get-tuple-element.22.refs_2_), channel_id=1, source_target_pairs={{0,8},{8,0},{16,24},{24,16},{1,9},{9,1},{17,25},{25,17},{2,10},{10... | collective-permute-start | bytes 393224 | tf_op jit(solution)/shard_map/ppermute | solution.py:219
  33.4 7.8 %collective-permute-start.4 = (bf16[16,4096]{1,0:T(8,128)(2,1)S(1)}, bf16[16,4096]{1,0:T(8,128)(2,1)S(1)}, u32[]{:S(2)}, u32[]{:S(2)}) collective-permute-start(bf16[16,4096]{1,0:T(8,128)(2,1)S(1)} %fusion.2.refs_1_), channel_id=1, source_target_pairs={{0,16},{8,24},{16,0},{24,8},{1,17},{9,25},{17,1},{25,9},{2,18},{10... | collective-permute-start | bytes 393224 | tf_op jit(solution)/shard_map/ppermute | solution.py:219
  41.6 5.6 %collective-permute-start.5 = (bf16[16,4096]{1,0:T(8,128)(2,1)S(1)}, bf16[16,4096]{1,0:T(8,128)(2,1)S(1)}, u32[]{:S(2)}, u32[]{:S(2)}) collective-permute-start(bf16[16,4096]{1,0:T(8,128)(2,1)S(1)} %multiply_convert_fusion), channel_id=1, source_target_pairs={{0,2},{1,3},{2,0},{3,1},{4,6},{5,7},{6,4},{7,5},{8,10},{9,11},{10,... | collective-permute-start | bytes 393224 | tf_op jit(solution)/shard_map/ppermute | solution.py:219
  42.7 7.8 %collective-permute-start.6 = (bf16[16,4096]{1,0:T(8,128)(2,1)S(1)}, bf16[16,4096]{1,0:T(8,128)(2,1)S(1)}, u32[]{:S(2)}, u32[]{:S(2)}) collective-permute-start(bf16[16,4096]{1,0:T(8,128)(2,1)S(1)} %multiply_convert_fusion), channel_id=1, source_target_pairs={{0,4},{1,5},{2,6},{3,7},{4,0},{5,1},{6,2},{7,3},{8,12},{9,13},{10,... | collective-permute-start | bytes 393224 | tf_op jit(solution)/shard_map/ppermute | solution.py:219
  43.2 7.2 %collective-permute-start.7 = (bf16[16,4096]{1,0:T(8,128)(2,1)S(1)}, bf16[16,4096]{1,0:T(8,128)(2,1)S(1)}, u32[]{:S(2)}, u32[]{:S(2)}) collective-permute-start(bf16[16,4096]{1,0:T(8,128)(2,1)S(1)} %multiply_convert_fusion), channel_id=1, source_target_pairs={{0,6},{1,7},{2,4},{3,5},{4,2},{5,3},{6,0},{7,1},{8,14},{9,15},{10,... | collective-permute-start | bytes 393224 | tf_op jit(solution)/shard_map/ppermute | solution.py:219
  50.5 4.2 %collective-permute-start.8 = (bf16[64,4096]{1,0:T(8,128)(2,1)S(1)}, bf16[64,4096]{1,0:T(8,128)(2,1)S(1)}, u32[]{:S(2)}, u32[]{:S(2)}) collective-permute-start(bf16[64,4096]{1,0:T(8,128)(2,1)S(1)} %pad_maximum_fusion.rows_ref), channel_id=1, source_target_pairs={{0,1},{1,0},{2,3},{3,2},{4,5},{5,4},{6,7},{7,6},{8,9},{9,8},{10,11... | collective-permute-start | bytes 1572872 | tf_op jit(solution)/shard_map/ppermute | solution.py:219
  56.7 6.8 %collective-permute-start.10 = (bf16[80,512]{1,0:T(8,128)(2,1)S(1)}, bf16[80,512]{1,0:T(8,128)(2,1)S(1)}, u32[]{:S(2)}, u32[]{:S(2)}) collective-permute-start(bf16[80,512]{1,0:T(8,128)(2,1)S(1)} %convolution_convert_fusion.refs_1_), channel_id=1, source_target_pairs={{0,16},{8,24},{16,0},{24,8},{1,17},{9,25},{17,1},{25,9},{2,18},{10... | collective-permute-start | bytes 245768 | tf_op jit(solution)/shard_map/ppermute | solution.py:219
  56.7 7.2 %collective-permute-start.11 = (bf16[80,512]{1,0:T(8,128)(2,1)S(1)}, bf16[80,512]{1,0:T(8,128)(2,1)S(1)}, u32[]{:S(2)}, u32[]{:S(2)}) collective-permute-start(bf16[80,512]{1,0:T(8,128)(2,1)S(1)} %convolution_convert_fusion.refs_1_), channel_id=1, source_target_pairs={{0,8},{8,0},{16,24},{24,16},{1,9},{9,1},{17,25},{25,17},{2,10},{10... | collective-permute-start | bytes 245768 | tf_op jit(solution)/shard_map/ppermute | solution.py:219
  58.2 7.3 %collective-permute-start.9 = (bf16[80,512]{1,0:T(8,128)(2,1)S(1)}, bf16[80,512]{1,0:T(8,128)(2,1)S(1)}, u32[]{:S(2)}, u32[]{:S(2)}) collective-permute-start(bf16[80,512]{1,0:T(8,128)(2,1)S(1)} %convolution_convert_fusion.refs_1_), channel_id=1, source_target_pairs={{0,24},{8,16},{16,8},{24,0},{1,25},{9,17},{17,9},{25,1},{2,26},{10... | collective-permute-start | bytes 245768 | tf_op jit(solution)/shard_map/ppermute | solution.py:219
  67.9 1.4 %collective-permute-start.12 = (bf16[64,1024]{1,0:T(8,128)(2,1)S(1)}, bf16[64,1024]{1,0:T(8,128)(2,1)S(1)}, u32[]{:S(2)}, u32[]{:S(2)}) collective-permute-start(bf16[64,1024]{1,0:T(8,128)(2,1)S(1)} %get-tuple-element.26), channel_id=1, source_target_pairs={{0,1},{1,0},{2,3},{3,2},{4,5},{5,4},{6,7},{7,6},{8,9},{9,8},{10,11... | collective-permute-start | bytes 393224 | tf_op jit(solution)/shard_map/ppermute | solution.py:219
  69.4 4.0 %collective-permute-start.13 = (bf16[16,1024]{1,0:T(8,128)(2,1)S(1)}, bf16[16,1024]{1,0:T(8,128)(2,1)S(1)}, u32[]{:S(2)}, u32[]{:S(2)}) collective-permute-start(bf16[16,1024]{1,0:T(8,128)(2,1)S(1)} %get-tuple-element.35), channel_id=1, source_target_pairs={{0,2},{1,3},{2,0},{3,1},{4,6},{5,7},{6,4},{7,5},{8,10},{9,11},{10,... | collective-permute-start | bytes 98312 | tf_op jit(solution)/shard_map/ppermute | solution.py:219
  70.4 3.9 %collective-permute-start.14 = (bf16[16,1024]{1,0:T(8,128)(2,1)S(1)}, bf16[16,1024]{1,0:T(8,128)(2,1)S(1)}, u32[]{:S(2)}, u32[]{:S(2)}) collective-permute-start(bf16[16,1024]{1,0:T(8,128)(2,1)S(1)} %get-tuple-element.37), channel_id=1, source_target_pairs={{0,4},{1,5},{2,6},{3,7},{4,0},{5,1},{6,2},{7,3},{8,12},{9,13},{10,... | collective-permute-start | bytes 98312 | tf_op jit(solution)/shard_map/ppermute | solution.py:219
  71.4 4.8 %collective-permute-start.15 = (bf16[16,1024]{1,0:T(8,128)(2,1)S(1)}, bf16[16,1024]{1,0:T(8,128)(2,1)S(1)}, u32[]{:S(2)}, u32[]{:S(2)}) collective-permute-start(bf16[16,1024]{1,0:T(8,128)(2,1)S(1)} %get-tuple-element.36), channel_id=1, source_target_pairs={{0,6},{1,7},{2,4},{3,5},{4,2},{5,3},{6,0},{7,1},{8,14},{9,15},{10,... | collective-permute-start | bytes 98312 | tf_op jit(solution)/shard_map/ppermute | solution.py:219
